TPU v7x, 256 devices: a whole 4x4x8 slice. The times are simulated.
256 devices in a mesh: expert: 64 (over z, y, core), tensor: 4 (over x).
Axes of the slice: x: 4, y: 4, z: 8, core: 2. Of those that a mesh axis runs over, the one named last changes fastest.
Arguments:
- context: bfloat16 [8192, 4096], P('expert', 'tensor'), may hold values from -6 to 6
- residual_in: bfloat16 [8192, 4096], P('expert')
- out_weight: bfloat16 [4096, 4096], P('tensor', 'expert'), may hold values from -0.09375 to 0.09375
- norm_gain: bfloat16 [4096], replicated, may hold values from 0.099609375 to 1.8984375
- expert_ids: int32 [8192, 8], P('expert'), may hold values from 0 to 63, all different within a row; in each aligned block of 128 rows (0 to 127, 128 to 255, ...) at most 18 rows name the same one
- gate_weights: float32 [8192, 8], P('expert'), may hold values from 0.1 to 1
- gate_matrix: bfloat16 [64, 4096, 1536], P('expert', None, 'tensor'), may hold values from -0.09375 to 0.09375
- lift_matrix: bfloat16 [64, 4096, 1536], P('expert', None, 'tensor'), may hold values from -0.09375 to 0.09375
- down_matrix: bfloat16 [64, 1536, 4096], P('expert', 'tensor'), may hold values from -0.15625 to 0.15625
Outputs:
- layer_out: bfloat16 [8192, 4096], P('expert', 'tensor')
Inputs may be any that keep to these rules, and one draw needn't show every extreme that they name: `expert_ids`: each row names 8 different experts. Within each aligned block of 128 rows (the rows of one index of the expert axis) no expert is named more than 18 times, a bound that some block reaches.
All inputs are finite; a program needn't handle non-finite values.
Results may differ from a plain program's by a relative error of at most 0.009.
Values may be sent and summed in bfloat16 or wider, within the bound.
No kernel may reach another device: no remote copies, remote signals or barrier semaphores. Data moves between devices by JAX's collectives and lax.ppermute only.
A program may use at most 128 MiB of HBM per device.

v0:
```python
import functools

import jax
import jax.numpy as jnp
from jax import lax
from jax.experimental import pallas as pl
from jax.experimental.pallas import tpu as pltpu
from jax.sharding import Mesh
from jax.sharding import PartitionSpec as P

epsilon = 1e-06
f32 = jnp.float32
bf16 = jnp.bfloat16
NZ, NY, NC, NX = 8, 4, 2, 4
NE = NZ * NY * NC
STEPS = (0, 1, 3, 2)
GROUPS = ((0, 1, -1), (4,), (3, -3), (2, -2))
SHIFTS = sum(GROUPS, ())
RING = (0, 1, -1, 2, -2, 3, -3)
TABLE = 32
BY_ROWS = (((0,), (0,)), ((), ()))
BY_COLUMNS = (((1,), (1,)), ((), ()))


def shape(*dims, dtype=bf16):
    return jax.ShapeDtypeStruct(dims, dtype)


def call(kernel, name, outs, *args, scratch=(), mib=24, flops=0, grid=(), specs=None):
    size = sum(a.size * a.dtype.itemsize for a in args)
    blocks = {} if specs is None else dict(grid=grid, in_specs=specs[0], out_specs=specs[1])
    return pl.pallas_call(
        kernel,
        out_shape=outs,
        scratch_shapes=scratch,
        **blocks,
        compiler_params=pltpu.CompilerParams(vmem_limit_bytes=mib << 20),
        cost_estimate=pl.CostEstimate(flops=flops, bytes_accessed=size, transcendentals=0),
        name=name,
    )(*args)


def shift(value, axis, count, step):
    if step % count == 0:
        return value
    return lax.ppermute(value, axis, [(i, (i + step) % count) for i in range(count)])


def y_exchange(values):
    return [shift(v, "y", NY, s) for v, s in zip(values, STEPS)]


def x_exchange(values):
    return [shift(v, "x", NX, s) for v, s in zip(values, STEPS)]


def swap(value):
    return shift(value, "c", NC, 1)


def x_ring(value, way):
    right, left = shift(value, "x", NX, 1), shift(value, "x", NX, -1)
    right, left = lax.optimization_barrier((right, left))
    far = shift(right, "x", NX, 1) if way else shift(left, "x", NX, -1)
    return value, right, left, far


def z_ring(value):
    right = left = value
    pieces = [value]
    for _ in range(NZ // 2 - 1):
        right, left = shift(right, "z", NZ, 1), shift(left, "z", NZ, -1)
        pieces += [right, left]
    half = value.shape[0] // 2
    return pieces + [shift(right[:half], "z", NZ, 1), shift(left[half:], "z", NZ, -1)]


def route_kernel(ids_ref, gates_ref, residual_ref, *outs):
    tokens = ids_ref.shape[1]
    x, y = lax.axis_index("x"), lax.axis_index("y")
    row = lax.broadcasted_iota(jnp.int32, (NE, tokens), 0)
    group = row // (NC * NZ)
    step = group ^ (group >> 1)
    experts = (row % NZ) * (NY * NC) + ((y + step) % NY) * NC + (row // NZ) % NC
    chosen = jnp.zeros((NE, tokens), f32)
    weight = jnp.zeros((NE, tokens), f32)
    for k in range(ids_ref.shape[0]):
        same = experts == ids_ref[k : k + 1, :]
        chosen = jnp.where(same, 1.0, chosen)
        weight = jnp.where(same, gates_ref[k : k + 1, :], weight)
    rows = lax.broadcasted_iota(jnp.int32, (tokens, tokens), 0)
    columns = lax.broadcasted_iota(jnp.int32, (tokens, tokens), 1)
    before = jnp.where(rows < columns, 1.0, 0.0).astype(bf16)
    rank = jnp.dot(chosen.astype(bf16), before, preferred_element_type=f32)
    slot = jnp.where(chosen > 0.0, rank, -1.0)
    high = weight.astype(bf16).astype(f32)
    low = weight - high
    share = residual_ref.shape[1] // NX
    half, piece = share // 2, share // 8
    for i, (s, out_ref) in enumerate(zip(STEPS, outs)):
        there = lax.rem(y + s, NY)
        for b in range(2):
            column = pl.multiple_of(x * share + b * half + there * piece, piece)
            out_ref[:tokens, b * piece : (b + 1) * piece] = residual_ref[:, pl.ds(column, piece)]
        for c in range(NC):
            at = (i * NC + c) * NZ
            part = [t[at : at + NZ] for t in (slot, high, low)]
            part.append(jnp.zeros((NZ, tokens), f32))
            part = jnp.concatenate(part, axis=0).astype(bf16)
            out_ref[tokens:, c * tokens : (c + 1) * tokens] = part


def project_kernel(*refs):
    contexts, (mine_ref, other_ref), outs = refs[:NY], refs[NY : NY + 2], refs[NY + 2 : -1]
    all_ref = refs[-1]
    width = all_ref.shape[1] // NC
    x, z, c = lax.axis_index("x"), lax.axis_index("z"), lax.axis_index("c")
    for i in range(NZ):
        owner = lax.rem(z + NZ - (RING + (4,))[i], NZ)
        for ref, core in ((mine_ref, c), (other_ref, 1 - c)):
            there = pl.ds(pl.multiple_of(core * width, width), width)
            all_ref[owner, there, :] = ref[i * width : (i + 1) * width, :]
    for step, out_ref in zip(STEPS, outs):
        q = lax.rem(x + step, NX)
        weight = all_ref[pl.ds(2 * q, 2)].reshape(out_ref.shape[2], -1)
        for i, ref in enumerate(contexts):
            part = lax.dot_general(ref[...], weight, BY_COLUMNS, preferred_element_type=f32)
            out_ref[i] = part.astype(out_ref.dtype)


def hidden_kernel(*refs):
    parts, packed, out_ref = refs[:NX], refs[NX : NX + NY], refs[NX + NY]
    tokens = parts[0].shape[1]
    y = lax.axis_index("y")
    for i, s in enumerate(STEPS):
        total = parts[0][i]
        for ref in parts[1:]:
            total = total + ref[i].astype(f32)
        owner = lax.rem(y + NY - s, NY)
        residual = packed[i][:tokens, :].astype(f32)
        out_ref[pl.ds(pl.multiple_of(owner * tokens, tokens), tokens), :] = (
            residual + total
        ).astype(bf16)


def fill_table(packed, other_ref, table_ref):
    tokens = table_ref.shape[2]
    y, c = lax.axis_index("y"), lax.axis_index("c")
    mine = pl.ds(pl.multiple_of(c * tokens, tokens), tokens)
    for i, s in enumerate(STEPS):
        owner = lax.rem(y + NY - s, NY)
        table_ref[owner] = packed[i][-TABLE:, mine].astype(f32)
        table_ref[owner + NY] = other_ref[i].astype(f32)


def pick_kernel(*refs):
    packed, out_ref = refs[:NY], refs[NY]
    tokens = out_ref.shape[2]
    c = lax.axis_index("c")
    others = pl.ds(pl.multiple_of((1 - c) * tokens, tokens), tokens)
    for i in range(NY):
        out_ref[i] = packed[i][-TABLE:, others]


def gather_kernel(*refs):
    pieces, out_ref = refs[:NY], refs[NY]
    y = lax.axis_index("y")
    piece = pieces[0].shape[1] // 2
    half = out_ref.shape[1] // 2
    for ref, s in zip(pieces, STEPS):
        owner = lax.rem(y + NY - s, NY)
        for b in range(2):
            column = pl.multiple_of(b * half + owner * piece, piece)
            out_ref[:, pl.ds(column, piece)] = ref[:, b * piece : (b + 1) * piece]


def dispatch_kernel(capacity, *refs):
    packed, other_ref = refs[:NY], refs[NY]
    hidden_ref, across_ref = refs[NY + 1 : NY + 3]
    sent, (own_ref, table_out, table_ref) = refs[NY + 3 : -3], refs[-3:]
    tokens = own_ref.shape[0]
    blocks = NY * NC
    y, z = lax.axis_index("y"), lax.axis_index("z")
    fill_table(packed, other_ref, table_ref)
    table_out[...] = table_ref[...]
    own_ref[...] = hidden_ref[pl.ds(pl.multiple_of(y * tokens, tokens), tokens), :]
    slots = lax.broadcasted_iota(jnp.int32, (blocks * capacity, NY * tokens), 0)
    for s, out_ref in zip(SHIFTS, sent):
        d = lax.rem(z + NZ + s, NZ)
        rows = None
        for core, ref in enumerate((hidden_ref, across_ref)):
            parts = []
            for b in range(core * NY, core * NY + NY):
                slot = table_ref[b, pl.ds(d, 1), :]
                parts.append(jnp.where(slot >= 0.0, slot + float(b * capacity), -1.0))
            place = jnp.concatenate(parts, axis=1).astype(jnp.int32)
            pick = jnp.where(slots == place, 1.0, 0.0).astype(bf16)
            part = jnp.dot(pick, ref[...], preferred_element_type=f32)
            rows = part if rows is None else rows + part
        out_ref[...] = rows.astype(bf16)


def join_kernel(*refs):
    row = 0
    for ref in refs[:-1]:
        refs[-1][row : row + ref.shape[0], :] = ref[...]
        row += ref.shape[0]


def cut_kernel(down_ref, *outs):
    share = outs[0].shape[1]
    x = lax.axis_index("x")
    for s, out_ref in zip(STEPS, outs):
        first = pl.multiple_of(lax.rem(x + s, NX) * share, share)
        out_ref[...] = down_ref[:, pl.ds(first, share)]


def up_kernel(width, *refs):
    pieces, (gain_ref, gate_ref, lift_ref, out_ref) = refs[:NX], refs[NX:]
    x = lax.axis_index("x")
    squares = None
    for ref in pieces:
        h = ref[...].astype(f32)
        s = jnp.sum(h * h, axis=1, keepdims=True)
        squares = s if squares is None else squares + s
    scale = lax.rsqrt(squares * (1.0 / width) + epsilon)
    gate = lift = None
    for ref, back in zip(pieces, STEPS):
        q = lax.rem(x + NX - back, NX)
        normed = (ref[...].astype(f32) * scale * gain_ref[pl.ds(q, 1), :]).astype(bf16)
        g = jnp.dot(normed, gate_ref[q], preferred_element_type=f32)
        l = jnp.dot(normed, lift_ref[q], preferred_element_type=f32)
        gate = g if gate is None else gate + g
        lift = l if lift is None else lift + l
    out_ref[...] = (gate / (1.0 + jnp.exp(-gate)) * lift).astype(bf16)


def down_kernel(*refs):
    acts, downs, outs = refs[:NX], refs[NX : 2 * NX], refs[2 * NX :]
    total = None
    for act, down in zip(acts, downs):
        part = jnp.dot(act[...], down[...], preferred_element_type=f32)
        part = part.astype(bf16).astype(f32)
        total = part if total is None else total + part
    total = total.astype(bf16)
    rows = outs[0].shape[0]
    for i, out in enumerate(outs):
        out[...] = total[i * rows : (i + 1) * rows]


def combine_kernel(capacity, start, shifts, table_ref, *refs):
    lists, rest, out_ref = refs[: len(shifts)], refs[len(shifts) : -1], refs[-1]
    tokens = table_ref.shape[2]
    block = pl.program_id(0) + start
    z = lax.axis_index("z")
    first = (block * capacity) // 16 * 16
    window = pl.ds(pl.multiple_of(first, 16), 32)
    slots = lax.broadcasted_iota(jnp.int32, (32, tokens), 0) - (block * capacity - first)
    slots = slots.astype(f32)
    spread, rows = [], []
    for s, ref in zip(shifts, lists):
        d = lax.rem(z + NZ + s, NZ)
        hit = (slots == table_ref[0, pl.ds(d, 1), :]) & (slots >= 0.0)
        for part in (1, 2):
            gate = table_ref[0, pl.ds(part * NZ + d, 1), :]
            spread.append(jnp.where(hit, gate, 0.0))
            rows.append(ref[window, :])
    total = lax.dot_general(
        jnp.concatenate(spread, axis=0).astype(bf16),
        jnp.concatenate(rows, axis=0),
        BY_ROWS,
        preferred_element_type=f32,
    )
    if rest:
        total = total + rest[0][0]
    out_ref[0] = total.astype(out_ref.dtype)


def merge_kernel(own_ref, got_ref, *outs):
    y = lax.axis_index("y")
    for s, out_ref in zip(STEPS, outs):
        there = lax.rem(y + s, NY)
        out_ref[...] = (own_ref[there] + got_ref[there].astype(f32)).astype(out_ref.dtype)


def final_kernel(hidden_ref, *refs):
    total = refs[0][...]
    for ref in refs[1:-1]:
        total = total + ref[...].astype(f32)
    refs[-1][...] = (hidden_ref[...].astype(f32) + total).astype(bf16)


def body(
    context,
    residual_in,
    out_weight,
    norm_gain,
    expert_ids,
    gate_weights,
    gate_matrix,
    lift_matrix,
    down_matrix,
):
    tokens, width = residual_in.shape
    top = expert_ids.shape[1]
    share = width // NX
    fine = share // NY
    units = gate_matrix.shape[2]
    capacity = min(tokens, max(2, tokens * top * 9 // (8 * NE)))
    blocks = NY * NC
    slots = blocks * capacity
    contexts = [shift(context, "y", NY, s) for s in STEPS]
    weight = jnp.concatenate(z_ring(out_weight.T), axis=0)
    packed = call(
        route_kernel,
        "route",
        [shape(tokens + TABLE, fine)] * NY,
        expert_ids.T,
        gate_weights.T,
        residual_in,
    )
    down_here, weight = lax.optimization_barrier((down_matrix[0], weight))
    downs = call(cut_kernel, "cut", [shape(units, share)] * NX, down_here)
    gain = norm_gain.astype(f32).reshape(NX, share)
    gain, contexts[0] = lax.optimization_barrier((gain, contexts[0]))
    weight, contexts = lax.optimization_barrier((weight, contexts))
    parts = call(
        project_kernel,
        "project",
        [shape(NY, tokens, fine, dtype=f32)] + [shape(NY, tokens, fine)] * (NX - 1),
        *contexts,
        weight,
        swap(weight),
        scratch=[pltpu.VMEM((NZ, NC * weight.shape[0] // NZ, share), bf16)],
        flops=2 * NY * tokens * share * width // NY,
    )
    parts, packed = lax.optimization_barrier((parts, packed))
    parts = x_exchange(parts)
    packed = y_exchange(packed)
    table = swap(call(pick_kernel, "pick", shape(NY, TABLE, tokens), *packed))
    parts, table, downs = lax.optimization_barrier((parts, table, downs))
    downs = x_exchange(downs)
    hidden = call(hidden_kernel, "hidden", shape(NY * tokens, fine), *parts, *packed)
    pieces = [shift(hidden, "y", NY, s) for s in STEPS]
    pieces, downs[1:3] = lax.optimization_barrier((pieces, downs[1:3]))
    hidden = call(gather_kernel, "gather", shape(NY * tokens, share), *pieces)
    *sent, own, table = call(
        functools.partial(dispatch_kernel, capacity),
        "dispatch",
        [shape(slots, share)] * NZ
        + [shape(tokens, share), shape(blocks, TABLE, tokens, dtype=f32)],
        *packed,
        table,
        hidden,
        swap(hidden),
        scratch=[pltpu.VMEM((blocks, TABLE, tokens), f32)],
        flops=2 * NZ * slots * blocks * tokens * share,
    )

    gate_here = gate_matrix.reshape(NX, share, units)
    lift_here = lift_matrix.reshape(NX, share, units)

    sent = dict(zip(SHIFTS, sent))
    got, rings, acts = [], [], []
    for i, group in enumerate(GROUPS):
        rows = [sent[s] for s in group]
        if i == 1:
            *rows, got[0] = lax.optimization_barrier((*rows, got[0]))
        elif i > 1:
            at, right, left, far = rings[i - 2]
            *rows, right, left = lax.optimization_barrier((*rows, right, left))
            rings[i - 2] = at, right, left, far
        rows = [shift(r, "z", NZ, s) for r, s in zip(rows, group)]
        if i > 1:
            at, right, left, far = rings[i - 2]
            *rows, far = lax.optimization_barrier((*rows, far))
            rings[i - 2] = at, right, left, far
        count = len(group) * slots
        got.append(rows[0] if len(rows) == 1 else call(join_kernel, f"join{i}", shape(count, share), *rows, mib=8))
        if i > 0:
            rings.append(x_ring(got[i - 1], i - 1 in (0, 3)))
    rings.append(x_ring(got[-1], True))
    for i, ring in enumerate(rings):
        count = ring[0].shape[0]
        acts.append(
            call(
                functools.partial(up_kernel, width),
                f"up{i}",
                shape(count, units),
                *ring,
                gain,
                gate_here,
                lift_here,
                flops=4 * count * width * units,
            )
        )
    acts[0], downs[3] = lax.optimization_barrier((acts[0], downs[3]))
    total = None
    for i, group in enumerate(GROUPS):
        count = got[i].shape[0]
        back = call(
            down_kernel,
            f"down{i}",
            [shape(slots, share)] * len(group),
            *x_ring(acts[i], i in (0, 3)),
            *downs,
            flops=2 * count * NX * units * share,
            grid=(share // 256,),
            specs=(
                [pl.BlockSpec((count, units), lambda i: (0, 0))] * NX
                + [pl.BlockSpec((units, 256), lambda i: (0, i))] * NX,
                [pl.BlockSpec((slots, 256), lambda i: (0, i))] * len(group),
            ),
        )
        lists = [shift(r, "z", NZ, -s) for r, s in zip(back, group)]

        def combine(start, number, dtype, total=total, lists=lists, group=group, i=i):
            part = pl.BlockSpec((1, tokens, share), lambda b: (b, 0, 0))
            there = pl.BlockSpec((1, tokens, share), lambda b: (b + start, 0, 0))
            return call(
                functools.partial(combine_kernel, capacity, start, group),
                f"combine{i}_{start}",
                shape(number, tokens, share, dtype=dtype),
                table,
                *lists,
                *([] if total is None else [total]),
                flops=4 * len(group) * number * 32 * tokens * share,
                grid=(number,),
                specs=(
                    [pl.BlockSpec((1, TABLE, tokens), lambda b: (b + start, 0, 0))]
                    + [pl.BlockSpec((slots, share), lambda b: (0, 0))] * len(group)
                    + ([] if total is None else [there]),
                    part,
                ),
            )

        if i < len(GROUPS) - 1:
            total = combine(0, blocks, f32)
    crossing = combine(NY, NY, bf16)
    mine = combine(0, NY, f32)
    merged = call(
        merge_kernel,
        "merge",
        [shape(tokens, share, dtype=f32)] + [shape(tokens, share)] * (NY - 1),
        mine,
        swap(crossing),
    )
    return call(final_kernel, "final", shape(tokens, share), own, *y_exchange(merged))


def solution(mesh):
    fine = Mesh(mesh.devices.reshape(NZ, NY, NC, NX), ("z", "y", "c", "x"))
    e = ("z", "y", "c")
    placed = (
        P(e, "x"),
        P(e, None),
        P("x", e),
        P(),
        P(e, None),
        P(e, None),
        P(e, None, "x"),
        P(e, None, "x"),
        P(e, "x", None),
    )
    return jax.shard_map(body, mesh=fine, in_specs=placed, out_specs=P(e, "x"), check_vma=False)
```

profile of v0, /device:TPU:1, one launch (start us, length us, event | category | flops | bytes accessed | tf_op | source)
XLA Modules:
  0.0 317.9 jit_solution(3042174611485302216)
XLA Ops:
  0.0 6.4 %collective-permute-start.1 = (bf16[64,1024]{1,0:T(8,128)(2,1)}, bf16[64,1024]{1,0:T(8,128)(2,1)S(1)}, u32[]{:S(2)}, u32[]{:S(2)}) collective-permute-start(bf16[64,1024]{1,0:T(8,128)(2,1)} %bitcast.18), channel_id=1, source_target_pairs={{0,224},{32,0},{64,32},{96,64},{128,96},{160,128},{192,160},{224,1... | collective-permute-start | bytes 393224 | tf_op jit(solution)/shard_map/ppermute | solution.py:46
  7.7 2.6 collective-permute-start.10
  13.0 2.8 collective-permute-start.3
  17.7 3.1 collective-permute-start.5
  22.8 3.2 collective-permute-start.7
  26.2 4.3 %collective-permute-done.6 = bf16[32,1024]{1,0:T(8,128)(2,1)S(1)} collective-permute-done((bf16[32,1024]{1,0:T(8,128)(2,1)S(1)}, bf16[32,1024]{1,0:T(8,128)(2,1)S(1)}, u32[]{:S(2)}, u32[]{:S(2)}) %collective-permute-start.6) | collective-permute-done | bytes 65568 | tf_op jit(solution)/shard_map/ppermute | solution.py:46
  30.6 5.7 %collective-permute-start.11 = (bf16[512,1024]{1,0:T(8,128)(2,1)S(1)}, bf16[512,1024]{1,0:T(8,128)(2,1)S(1)}, u32[]{:S(2)}, u32[]{:S(2)}) collective-permute-start(bf16[512,1024]{1,0:T(8,128)(2,1)S(1)} %constant_dynamic-update-slice_fusion.refs_4_), channel_id=1, source_target_pairs={{0,4},{4,0},{1,5},{5,1},{2,6},{6,2},{3,7},{7,3},{8,12},{12,8},{9,1... | collective-permute-start | bytes 3145736 | tf_op jit(solution)/shard_map/ppermute | solution.py:46
  39.1 2.9 project.1
  51.4 5.1 %collective-permute-done.14.refs_3_.refs_7_ = bf16[160,256]{1,0:T(8,128)(2,1)S(1)} collective-permute-done((bf16[160,256]{1,0:T(8,128)(2,1)S(1)}, bf16[160,256]{1,0:T(8,128)(2,1)S(1)}, u32[]{:S(2)}, u32[]{:S(2)}) %collective-permute-start.14) | collective-permute-done | bytes 81952 | tf_op jit(solution)/shard_map/ppermute | solution.py:46
  56.5 2.6 collective-permute-start.18
  64.5 6.9 %collective-permute-done.21.refs_3_ = bf16[512,256]{1,0:T(8,128)(2,1)S(1)} collective-permute-done((bf16[512,256]{1,0:T(8,128)(2,1)S(1)}, bf16[512,256]{1,0:T(8,128)(2,1)S(1)}, u32[]{:S(2)}, u32[]{:S(2)}) %collective-permute-start.21) | collective-permute-done | bytes 262176 | tf_op jit(solution)/shard_map/ppermute | solution.py:46
  71.4 2.9 collective-permute-done.20.refs_2_
  74.2 4.0 %collective-permute-done.19.refs_1_ = bf16[512,256]{1,0:T(8,128)(2,1)S(1)} collective-permute-done((bf16[512,256]{1,0:T(8,128)(2,1)S(1)}, bf16[512,256]{1,0:T(8,128)(2,1)S(1)}, u32[]{:S(2)}, u32[]{:S(2)}) %collective-permute-start.19) | collective-permute-done | bytes 262176 | tf_op jit(solution)/shard_map/ppermute | solution.py:46
  83.9 2.6 dispatch.1
  86.6 2.7 collective-permute-start.26
  89.3 6.8 %collective-permute-done.25.refs_1_ = bf16[144,1024]{1,0:T(8,128)(2,1)S(1)} collective-permute-done((bf16[144,1024]{1,0:T(8,128)(2,1)S(1)}, bf16[144,1024]{1,0:T(8,128)(2,1)S(1)}, u32[]{:S(2)}, u32[]{:S(2)}) %collective-permute-start.25) | collective-permute-done | bytes 294944 | tf_op jit(solution)/shard_map/ppermute | solution.py:46
  96.1 11.7 %collective-permute-start.40 = (bf16[432,1024]{1,0:T(8,128)(2,1)S(1)}, bf16[432,1024]{1,0:T(8,128)(2,1)S(1)}, u32[]{:S(2)}, u32[]{:S(2)}) collective-permute-start(bf16[432,1024]{1,0:T(8,128)(2,1)S(1)} %join0.1.refs_0_), channel_id=1, source_target_pairs={{0,3},{1,0},{2,1},{3,2},{4,7},{5,4},{6,5},{7,6},{8,11},{9,8},{10,9... | collective-permute-start | bytes 2654216 | tf_op jit(solution)/shard_map/ppermute | solution.py:46
  109.0 16.2 %collective-permute-done.27.refs_0_ = bf16[144,1024]{1,0:T(8,128)(2,1)S(1)} collective-permute-done((bf16[144,1024]{1,0:T(8,128)(2,1)S(1)}, bf16[144,1024]{1,0:T(8,128)(2,1)S(1)}, u32[]{:S(2)}, u32[]{:S(2)}) %collective-permute-start.27) | collective-permute-done | bytes 294944 | tf_op jit(solution)/shard_map/ppermute | solution.py:46
  125.2 2.5 collective-permute-start.29
  128.6 2.7 collective-permute-done.29.refs_2_
  131.4 3.1 collective-permute-done.28.refs_1_
  134.4 3.6 %collective-permute-start.31 = (bf16[144,1024]{1,0:T(8,128)(2,1)S(1)}, bf16[144,1024]{1,0:T(8,128)(2,1)S(1)}, u32[]{:S(2)}, u32[]{:S(2)}) collective-permute-start(bf16[144,1024]{1,0:T(8,128)(2,1)S(1)} %get-tuple-element.155), channel_id=1, source_target_pairs={{0,192},{32,224},{64,0},{96,32},{128,64},{160,96},{192,128},{224,1... | collective-permute-start | bytes 884744 | tf_op jit(solution)/shard_map/ppermute | solution.py:46
  138.4 3.1 collective-permute-start.41
  142.2 9.5 %collective-permute-start.42 = (bf16[144,1024]{1,0:T(8,128)(2,1)S(1)}, bf16[144,1024]{1,0:T(8,128)(2,1)S(1)}, u32[]{:S(2)}, u32[]{:S(2)}) collective-permute-start(bf16[144,1024]{1,0:T(8,128)(2,1)S(1)} %get-tuple-element.174), channel_id=1, source_target_pairs={{0,160},{32,192},{64,224},{96,0},{128,32},{160,64},{192,96},{224,1... | collective-permute-start | bytes 884744 | tf_op jit(solution)/shard_map/ppermute | solution.py:46
  153.6 11.2 %collective-permute-done.41.refs_0_ = bf16[144,1024]{1,0:T(8,128)(2,1)S(1)} collective-permute-done((bf16[144,1024]{1,0:T(8,128)(2,1)S(1)}, bf16[144,1024]{1,0:T(8,128)(2,1)S(1)}, u32[]{:S(2)}, u32[]{:S(2)}) %collective-permute-start.41) | collective-permute-done | bytes 294944 | tf_op jit(solution)/shard_map/ppermute | solution.py:46
  164.8 3.5 %collective-permute-start.48 = (bf16[288,1024]{1,0:T(8,128)(2,1)S(1)}, bf16[288,1024]{1,0:T(8,128)(2,1)S(1)}, u32[]{:S(2)}, u32[]{:S(2)}) collective-permute-start(bf16[288,1024]{1,0:T(8,128)(2,1)S(1)} %join2.1.refs_0_), channel_id=1, source_target_pairs={{0,3},{1,0},{2,1},{3,2},{4,7},{5,4},{6,5},{7,6},{8,11},{9,8},{10,9... | collective-permute-start | bytes 1769480 | tf_op jit(solution)/shard_map/ppermute | solution.py:46
  168.2 3.3 %collective-permute-start.44 = (bf16[384,1024]{1,0:T(8,128)(2,1)S(1)}, bf16[384,1024]{1,0:T(8,128)(2,1)S(1)}, u32[]{:S(2)}, u32[]{:S(2)}) collective-permute-start(bf16[384,1024]{1,0:T(8,128)(2,1)S(1)} %get-tuple-element.176), channel_id=1, source_target_pairs={{0,2},{1,3},{2,0},{3,1},{4,6},{5,7},{6,4},{7,5},{8,10},{9,11},{10,... | collective-permute-start | bytes 2359304 | tf_op jit(solution)/shard_map/ppermute | solution.py:46
  171.5 13.0 %collective-permute-done.48.refs_2_ = bf16[288,1024]{1,0:T(8,128)(2,1)S(1)} collective-permute-done((bf16[288,1024]{1,0:T(8,128)(2,1)S(1)}, bf16[288,1024]{1,0:T(8,128)(2,1)S(1)}, u32[]{:S(2)}, u32[]{:S(2)}) %collective-permute-start.48) | collective-permute-done | bytes 589856 | tf_op jit(solution)/shard_map/ppermute | solution.py:46
  184.5 4.3 %collective-permute-start.49 = (bf16[288,1024]{1,0:T(8,128)(2,1)S(1)}, bf16[288,1024]{1,0:T(8,128)(2,1)S(1)}, u32[]{:S(2)}, u32[]{:S(2)}) collective-permute-start(bf16[288,1024]{1,0:T(8,128)(2,1)S(1)} %collective-permute-done.48.refs_2_), channel_id=1, source_target_pairs={{0,3},{1,0},{2,1},{3,2},{4,7},{5,4},{6,5},{7,6},{8,11},{9,8},{10,9... | collective-permute-start | bytes 1769480 | tf_op jit(solution)/shard_map/ppermute | solution.py:46
  188.8 4.6 %up0.1.refs_0_ = bf16[432,384]{1,0:T(8,128)(2,1)S(1)} custom-call(bf16[432,1024]{1,0:T(8,128)(2,1)S(1)} %join0.1.refs_0_, bf16[432,1024]{1,0:T(8,128)(2,1)S(1)} %collective-permute-done.39.refs_1_, bf16[432,1024]{1,0:T(8,128)(2,1)S(1)} %collective-permute-done.40.refs_2_, bf16[432,1024]{1,0:T(8,128)(2,1)S(1)} %collective-permute-done.43.refs_3_, ...), custom_call_target="tpu_custom_call" | custom-call | flops 2717908992 | bytes 9846784 | tf_op jit(solution)/shard_map/up0/pallas_call | solution.py:32
  193.4 8.9 %collective-permute-done.44.refs_7_ = bf16[384,1024]{1,0:T(8,128)(2,1)S(1)} collective-permute-done((bf16[384,1024]{1,0:T(8,128)(2,1)S(1)}, bf16[384,1024]{1,0:T(8,128)(2,1)S(1)}, u32[]{:S(2)}, u32[]{:S(2)}) %collective-permute-start.44) | collective-permute-done | bytes 786464 | tf_op jit(solution)/shard_map/ppermute | solution.py:46
  206.8 3.1 collective-permute-done.35.refs_3_
  209.9 3.2 up3.1.refs_0_
  214.4 4.0 %collective-permute-start.37 = (bf16[288,384]{1,0:T(8,128)(2,1)S(1)}, bf16[288,384]{1,0:T(8,128)(2,1)S(1)}, u32[]{:S(2)}, u32[]{:S(2)}) collective-permute-start(bf16[288,384]{1,0:T(8,128)(2,1)S(1)} %up3.1.refs_0_), channel_id=1, source_target_pairs={{0,3},{1,0},{2,1},{3,2},{4,7},{5,4},{6,5},{7,6},{8,11},{9,8},{10,9... | collective-permute-start | bytes 663560 | tf_op jit(solution)/shard_map/ppermute | solution.py:46
  221.1 3.2 up2.1.refs_0_
  228.5 4.2 %collective-permute-done.51.refs_2_ = bf16[288,384]{1,0:T(8,128)(2,1)S(1)} collective-permute-done((bf16[288,384]{1,0:T(8,128)(2,1)S(1)}, bf16[288,384]{1,0:T(8,128)(2,1)S(1)}, u32[]{:S(2)}, u32[]{:S(2)}) %collective-permute-start.51) | collective-permute-done | bytes 221216 | tf_op jit(solution)/shard_map/ppermute | solution.py:46
  232.7 5.4 %collective-permute-done.50.refs_1_ = bf16[288,384]{1,0:T(8,128)(2,1)S(1)} collective-permute-done((bf16[288,384]{1,0:T(8,128)(2,1)S(1)}, bf16[288,384]{1,0:T(8,128)(2,1)S(1)}, u32[]{:S(2)}, u32[]{:S(2)}) %collective-permute-start.50) | collective-permute-done | bytes 221216 | tf_op jit(solution)/shard_map/ppermute | solution.py:46
  238.8 3.1 down0.1
  246.3 2.5 down2.1
  248.7 4.5 %collective-permute-start.53 = (bf16[144,1024]{1,0:T(8,128)(2,1)S(1)}, bf16[144,1024]{1,0:T(8,128)(2,1)S(1)}, u32[]{:S(2)}, u32[]{:S(2)}) collective-permute-start(bf16[144,1024]{1,0:T(8,128)(2,1)S(1)} %get-tuple-element.186), channel_id=1, source_target_pairs={{0,160},{32,192},{64,224},{96,0},{128,32},{160,64},{192,96},{224,1... | collective-permute-start | bytes 884744 | tf_op jit(solution)/shard_map/ppermute | solution.py:46
  253.3 2.5 down3.1
  255.7 3.6 %collective-permute-start.45 = (bf16[144,1024]{1,0:T(8,128)(2,1)S(1)}, bf16[144,1024]{1,0:T(8,128)(2,1)S(1)}, u32[]{:S(2)}, u32[]{:S(2)}) collective-permute-start(bf16[144,1024]{1,0:T(8,128)(2,1)S(1)} %get-tuple-element.178), channel_id=1, source_target_pairs={{0,192},{32,224},{64,0},{96,32},{128,64},{160,96},{192,128},{224,1... | collective-permute-start | bytes 884744 | tf_op jit(solution)/shard_map/ppermute | solution.py:46
  263.7 5.7 %collective-permute-done.53.refs_0_ = bf16[144,1024]{1,0:T(8,128)(2,1)S(1)} collective-permute-done((bf16[144,1024]{1,0:T(8,128)(2,1)S(1)}, bf16[144,1024]{1,0:T(8,128)(2,1)S(1)}, u32[]{:S(2)}, u32[]{:S(2)}) %collective-permute-start.53) | collective-permute-done | bytes 294944 | tf_op jit(solution)/shard_map/ppermute | solution.py:46
  269.4 2.9 collective-permute-done.54.refs_1_
  274.5 16.9 %collective-permute-done.45.refs_0_ = bf16[144,1024]{1,0:T(8,128)(2,1)S(1)} collective-permute-done((bf16[144,1024]{1,0:T(8,128)(2,1)S(1)}, bf16[144,1024]{1,0:T(8,128)(2,1)S(1)}, u32[]{:S(2)}, u32[]{:S(2)}) %collective-permute-start.45) | collective-permute-done | bytes 294944 | tf_op jit(solution)/shard_map/ppermute | solution.py:46
  292.5 7.4 %collective-permute-start.64 = (bf16[4,128,1024]{2,1,0:T(8,128)(2,1)S(1)}, bf16[4,128,1024]{2,1,0:T(8,128)(2,1)S(1)}, u32[]{:S(2)}, u32[]{:S(2)}) collective-permute-start(bf16[4,128,1024]{2,1,0:T(8,128)(2,1)S(1)} %combine3_4.1), channel_id=1, source_target_pairs={{0,4},{4,0},{1,5},{5,1},{2,6},{6,2},{3,7},{7,3},{8,12},{12,8},{9,1... | collective-permute-start | bytes 3145736 | tf_op jit(solution)/shard_map/ppermute | solution.py:46
  302.4 2.7 collective-permute-start.66
  305.1 11.7 %collective-permute-done.65.refs_1_ = bf16[128,1024]{1,0:T(8,128)(2,1)S(1)} collective-permute-done((bf16[128,1024]{1,0:T(8,128)(2,1)S(1)}, bf16[128,1024]{1,0:T(8,128)(2,1)S(1)}, u32[]{:S(2)}, u32[]{:S(2)}) %collective-permute-start.65) | collective-permute-done | bytes 262176 | tf_op jit(solution)/shard_map/ppermute | solution.py:46
  (139 shorter events, 65.5 us)
Async XLA Ops:
  0.0 13.0 %collective-permute-start.1 = (bf16[64,1024]{1,0:T(8,128)(2,1)}, bf16[64,1024]{1,0:T(8,128)(2,1)S(1)}, u32[]{:S(2)}, u32[]{:S(2)}) collective-permute-start(bf16[64,1024]{1,0:T(8,128)(2,1)} %bitcast.18), channel_id=1, source_target_pairs={{0,224},{32,0},{64,32},{96,64},{128,96},{160,128},{192,160},{224,1... | collective-permute-start | bytes 393224 | tf_op jit(solution)/shard_map/ppermute | solution.py:46
  6.4 24.1 %collective-permute-start.8 = (bf16[128,1024]{1,0:T(8,128)(2,1)}, bf16[128,1024]{1,0:T(8,128)(2,1)S(1)}, u32[]{:S(2)}, u32[]{:S(2)}) collective-permute-start(bf16[128,1024]{1,0:T(8,128)(2,1)} %refs_0_), channel_id=1, source_target_pairs={{0,8},{8,16},{16,24},{24,0},{1,9},{9,17},{17,25},{25,1},{2,10},{10... | collective-permute-start | bytes 786440 | tf_op jit(solution)/shard_map/ppermute | solution.py:46
  7.7 22.8 %collective-permute-start.10 = (bf16[128,1024]{1,0:T(8,128)(2,1)}, bf16[128,1024]{1,0:T(8,128)(2,1)S(1)}, u32[]{:S(2)}, u32[]{:S(2)}) collective-permute-start(bf16[128,1024]{1,0:T(8,128)(2,1)} %refs_0_), channel_id=1, source_target_pairs={{0,16},{8,24},{16,0},{24,8},{1,17},{9,25},{17,1},{25,9},{2,18},{10... | collective-permute-start | bytes 786440 | tf_op jit(solution)/shard_map/ppermute | solution.py:46
  10.3 20.2 %collective-permute-start.9 = (bf16[128,1024]{1,0:T(8,128)(2,1)}, bf16[128,1024]{1,0:T(8,128)(2,1)S(1)}, u32[]{:S(2)}, u32[]{:S(2)}) collective-permute-start(bf16[128,1024]{1,0:T(8,128)(2,1)} %refs_0_), channel_id=1, source_target_pairs={{0,24},{8,0},{16,8},{24,16},{1,25},{9,1},{17,9},{25,17},{2,26},{10... | collective-permute-start | bytes 786440 | tf_op jit(solution)/shard_map/ppermute | solution.py:46
  42.1 17.9 %collective-permute-start.15 = (bf16[4,128,256]{2,1,0:T(8,128)(2,1)S(1)}, bf16[4,128,256]{2,1,0:T(8,128)(2,1)S(1)}, u32[]{:S(2)}, u32[]{:S(2)}) collective-permute-start(bf16[4,128,256]{2,1,0:T(8,128)(2,1)S(1)} %get-tuple-element.124), channel_id=1, source_target_pairs={{0,1},{1,2},{2,3},{3,0},{4,5},{5,6},{6,7},{7,4},{8,9},{9,10},{10,1... | collective-permute-start | bytes 786440 | tf_op jit(solution)/shard_map/ppermute | solution.py:46
  43.4 16.6 %collective-permute-start.16 = (bf16[4,128,256]{2,1,0:T(8,128)(2,1)S(1)}, bf16[4,128,256]{2,1,0:T(8,128)(2,1)S(1)}, u32[]{:S(2)}, u32[]{:S(2)}) collective-permute-start(bf16[4,128,256]{2,1,0:T(8,128)(2,1)S(1)} %get-tuple-element.125), channel_id=1, source_target_pairs={{0,3},{1,0},{2,1},{3,2},{4,7},{5,4},{6,5},{7,6},{8,11},{9,8},{10,9... | collective-permute-start | bytes 786440 | tf_op jit(solution)/shard_map/ppermute | solution.py:46
  44.8 15.1 %collective-permute-start.17 = (bf16[4,128,256]{2,1,0:T(8,128)(2,1)S(1)}, bf16[4,128,256]{2,1,0:T(8,128)(2,1)S(1)}, u32[]{:S(2)}, u32[]{:S(2)}) collective-permute-start(bf16[4,128,256]{2,1,0:T(8,128)(2,1)S(1)} %get-tuple-element.126), channel_id=1, source_target_pairs={{0,2},{1,3},{2,0},{3,1},{4,6},{5,7},{6,4},{7,5},{8,10},{9,11},{10,... | collective-permute-start | bytes 786440 | tf_op jit(solution)/shard_map/ppermute | solution.py:46
  59.9 20.1 %collective-permute-start.22 = (bf16[384,1024]{1,0:T(8,128)(2,1)S(1)}, bf16[384,1024]{1,0:T(8,128)(2,1)S(1)}, u32[]{:S(2)}, u32[]{:S(2)}) collective-permute-start(bf16[384,1024]{1,0:T(8,128)(2,1)S(1)} %get-tuple-element.137), channel_id=1, source_target_pairs={{0,1},{1,2},{2,3},{3,0},{4,5},{5,6},{6,7},{7,4},{8,9},{9,10},{10,1... | collective-permute-start | bytes 2359304 | tf_op jit(solution)/shard_map/ppermute | solution.py:46
  60.3 19.7 %collective-permute-start.23 = (bf16[384,1024]{1,0:T(8,128)(2,1)S(1)}, bf16[384,1024]{1,0:T(8,128)(2,1)S(1)}, u32[]{:S(2)}, u32[]{:S(2)}) collective-permute-start(bf16[384,1024]{1,0:T(8,128)(2,1)S(1)} %get-tuple-element.138), channel_id=1, source_target_pairs={{0,3},{1,0},{2,1},{3,2},{4,7},{5,4},{6,5},{7,6},{8,11},{9,8},{10,9... | collective-permute-start | bytes 2359304 | tf_op jit(solution)/shard_map/ppermute | solution.py:46
  62.9 11.3 %collective-permute-start.20 = (bf16[512,256]{1,0:T(8,128)(2,1)S(1)}, bf16[512,256]{1,0:T(8,128)(2,1)S(1)}, u32[]{:S(2)}, u32[]{:S(2)}) collective-permute-start(bf16[512,256]{1,0:T(8,128)(2,1)S(1)} %hidden.1.refs_0_), channel_id=1, source_target_pairs={{0,24},{8,0},{16,8},{24,16},{1,25},{9,1},{17,9},{25,17},{2,26},{10... | collective-permute-start | bytes 786440 | tf_op jit(solution)/shard_map/ppermute | solution.py:46
  64.5 13.8 %collective-permute-start.19 = (bf16[512,256]{1,0:T(8,128)(2,1)S(1)}, bf16[512,256]{1,0:T(8,128)(2,1)S(1)}, u32[]{:S(2)}, u32[]{:S(2)}) collective-permute-start(bf16[512,256]{1,0:T(8,128)(2,1)S(1)} %hidden.1.refs_0_), channel_id=1, source_target_pairs={{0,8},{8,16},{16,24},{24,0},{1,9},{9,17},{17,25},{25,1},{2,10},{10... | collective-permute-start | bytes 786440 | tf_op jit(solution)/shard_map/ppermute | solution.py:46
  86.5 9.5 %collective-permute-start.25 = (bf16[144,1024]{1,0:T(8,128)(2,1)S(1)}, bf16[144,1024]{1,0:T(8,128)(2,1)S(1)}, u32[]{:S(2)}, u32[]{:S(2)}) collective-permute-start(bf16[144,1024]{1,0:T(8,128)(2,1)S(1)} %get-tuple-element.149), channel_id=1, source_target_pairs={{0,32},{32,64},{64,96},{96,128},{128,160},{160,192},{192,224},{224... | collective-permute-start | bytes 884744 | tf_op jit(solution)/shard_map/ppermute | solution.py:46
  86.6 9.4 %collective-permute-start.26 = (bf16[144,1024]{1,0:T(8,128)(2,1)S(1)}, bf16[144,1024]{1,0:T(8,128)(2,1)S(1)}, u32[]{:S(2)}, u32[]{:S(2)}) collective-permute-start(bf16[144,1024]{1,0:T(8,128)(2,1)S(1)} %get-tuple-element.150), channel_id=1, source_target_pairs={{0,224},{32,0},{64,32},{96,64},{128,96},{160,128},{192,160},{224,1... | collective-permute-start | bytes 884744 | tf_op jit(solution)/shard_map/ppermute | solution.py:46
  96.1 31.5 %collective-permute-start.40 = (bf16[432,1024]{1,0:T(8,128)(2,1)S(1)}, bf16[432,1024]{1,0:T(8,128)(2,1)S(1)}, u32[]{:S(2)}, u32[]{:S(2)}) collective-permute-start(bf16[432,1024]{1,0:T(8,128)(2,1)S(1)} %join0.1.refs_0_), channel_id=1, source_target_pairs={{0,3},{1,0},{2,1},{3,2},{4,7},{5,4},{6,5},{7,6},{8,11},{9,8},{10,9... | collective-permute-start | bytes 2654216 | tf_op jit(solution)/shard_map/ppermute | solution.py:46
  107.8 20.9 %collective-permute-start.39 = (bf16[432,1024]{1,0:T(8,128)(2,1)S(1)}, bf16[432,1024]{1,0:T(8,128)(2,1)S(1)}, u32[]{:S(2)}, u32[]{:S(2)}) collective-permute-start(bf16[432,1024]{1,0:T(8,128)(2,1)S(1)} %join0.1.refs_0_), channel_id=1, source_target_pairs={{0,1},{1,2},{2,3},{3,0},{4,5},{5,6},{6,7},{7,4},{8,9},{9,10},{10,1... | collective-permute-start | bytes 2654216 | tf_op jit(solution)/shard_map/ppermute | solution.py:46
  107.8 17.4 %collective-permute-start.27 = (bf16[144,1024]{1,0:T(8,128)(2,1)S(1)}, bf16[144,1024]{1,0:T(8,128)(2,1)S(1)}, u32[]{:S(2)}, u32[]{:S(2)}) collective-permute-start(bf16[144,1024]{1,0:T(8,128)(2,1)S(1)} %get-tuple-element.151), channel_id=1, source_target_pairs={{0,128},{32,160},{64,192},{96,224},{128,0},{160,32},{192,64},{224,... | collective-permute-start | bytes 884744 | tf_op jit(solution)/shard_map/ppermute | solution.py:46
  128.6 36.1 %collective-permute-start.43 = (bf16[432,1024]{1,0:T(8,128)(2,1)S(1)}, bf16[432,1024]{1,0:T(8,128)(2,1)S(1)}, u32[]{:S(2)}, u32[]{:S(2)}) collective-permute-start(bf16[432,1024]{1,0:T(8,128)(2,1)S(1)} %collective-permute-done.39.refs_1_), channel_id=1, source_target_pairs={{0,1},{1,2},{2,3},{3,0},{4,5},{5,6},{6,7},{7,4},{8,9},{9,10},{10,1... | collective-permute-start | bytes 2654216 | tf_op jit(solution)/shard_map/ppermute | solution.py:46
  134.4 17.3 %collective-permute-start.31 = (bf16[144,1024]{1,0:T(8,128)(2,1)S(1)}, bf16[144,1024]{1,0:T(8,128)(2,1)S(1)}, u32[]{:S(2)}, u32[]{:S(2)}) collective-permute-start(bf16[144,1024]{1,0:T(8,128)(2,1)S(1)} %get-tuple-element.155), channel_id=1, source_target_pairs={{0,192},{32,224},{64,0},{96,32},{128,64},{160,96},{192,128},{224,1... | collective-permute-start | bytes 884744 | tf_op jit(solution)/shard_map/ppermute | solution.py:46
  138.0 13.7 %collective-permute-start.32 = (bf16[144,1024]{1,0:T(8,128)(2,1)S(1)}, bf16[144,1024]{1,0:T(8,128)(2,1)S(1)}, u32[]{:S(2)}, u32[]{:S(2)}) collective-permute-start(bf16[144,1024]{1,0:T(8,128)(2,1)S(1)} %collective-permute-done.29.refs_2_), channel_id=1, source_target_pairs={{0,3},{1,0},{2,1},{3,2},{4,7},{5,4},{6,5},{7,6},{8,11},{9,8},{10,9... | collective-permute-start | bytes 884744 | tf_op jit(solution)/shard_map/ppermute | solution.py:46
  138.4 26.3 %collective-permute-start.41 = (bf16[144,1024]{1,0:T(8,128)(2,1)S(1)}, bf16[144,1024]{1,0:T(8,128)(2,1)S(1)}, u32[]{:S(2)}, u32[]{:S(2)}) collective-permute-start(bf16[144,1024]{1,0:T(8,128)(2,1)S(1)} %get-tuple-element.173), channel_id=1, source_target_pairs={{0,96},{32,128},{64,160},{96,192},{128,224},{160,0},{192,32},{224,... | collective-permute-start | bytes 884744 | tf_op jit(solution)/shard_map/ppermute | solution.py:46
  142.2 22.5 %collective-permute-start.42 = (bf16[144,1024]{1,0:T(8,128)(2,1)S(1)}, bf16[144,1024]{1,0:T(8,128)(2,1)S(1)}, u32[]{:S(2)}, u32[]{:S(2)}) collective-permute-start(bf16[144,1024]{1,0:T(8,128)(2,1)S(1)} %get-tuple-element.174), channel_id=1, source_target_pairs={{0,160},{32,192},{64,224},{96,0},{128,32},{160,64},{192,96},{224,1... | collective-permute-start | bytes 884744 | tf_op jit(solution)/shard_map/ppermute | solution.py:46
  151.7 19.8 %collective-permute-start.34 = (bf16[288,1024]{1,0:T(8,128)(2,1)S(1)}, bf16[288,1024]{1,0:T(8,128)(2,1)S(1)}, u32[]{:S(2)}, u32[]{:S(2)}) collective-permute-start(bf16[288,1024]{1,0:T(8,128)(2,1)S(1)} %join3.1.refs_0_), channel_id=1, source_target_pairs={{0,3},{1,0},{2,1},{3,2},{4,7},{5,4},{6,5},{7,6},{8,11},{9,8},{10,9... | collective-permute-start | bytes 1769480 | tf_op jit(solution)/shard_map/ppermute | solution.py:46
  153.6 18.0 %collective-permute-start.33 = (bf16[288,1024]{1,0:T(8,128)(2,1)S(1)}, bf16[288,1024]{1,0:T(8,128)(2,1)S(1)}, u32[]{:S(2)}, u32[]{:S(2)}) collective-permute-start(bf16[288,1024]{1,0:T(8,128)(2,1)S(1)} %join3.1.refs_0_), channel_id=1, source_target_pairs={{0,1},{1,2},{2,3},{3,0},{4,5},{5,6},{6,7},{7,4},{8,9},{9,10},{10,1... | collective-permute-start | bytes 1769480 | tf_op jit(solution)/shard_map/ppermute | solution.py:46
  164.8 19.7 %collective-permute-start.48 = (bf16[288,1024]{1,0:T(8,128)(2,1)S(1)}, bf16[288,1024]{1,0:T(8,128)(2,1)S(1)}, u32[]{:S(2)}, u32[]{:S(2)}) collective-permute-start(bf16[288,1024]{1,0:T(8,128)(2,1)S(1)} %join2.1.refs_0_), channel_id=1, source_target_pairs={{0,3},{1,0},{2,1},{3,2},{4,7},{5,4},{6,5},{7,6},{8,11},{9,8},{10,9... | collective-permute-start | bytes 1769480 | tf_op jit(solution)/shard_map/ppermute | solution.py:46
  168.2 16.2 %collective-permute-start.47 = (bf16[288,1024]{1,0:T(8,128)(2,1)S(1)}, bf16[288,1024]{1,0:T(8,128)(2,1)S(1)}, u32[]{:S(2)}, u32[]{:S(2)}) collective-permute-start(bf16[288,1024]{1,0:T(8,128)(2,1)S(1)} %join2.1.refs_0_), channel_id=1, source_target_pairs={{0,1},{1,2},{2,3},{3,0},{4,5},{5,6},{6,7},{7,4},{8,9},{9,10},{10,1... | collective-permute-start | bytes 1769480 | tf_op jit(solution)/shard_map/ppermute | solution.py:46
  168.2 34.0 %collective-permute-start.44 = (bf16[384,1024]{1,0:T(8,128)(2,1)S(1)}, bf16[384,1024]{1,0:T(8,128)(2,1)S(1)}, u32[]{:S(2)}, u32[]{:S(2)}) collective-permute-start(bf16[384,1024]{1,0:T(8,128)(2,1)S(1)} %get-tuple-element.176), channel_id=1, source_target_pairs={{0,2},{1,3},{2,0},{3,1},{4,6},{5,7},{6,4},{7,5},{8,10},{9,11},{10,... | collective-permute-start | bytes 2359304 | tf_op jit(solution)/shard_map/ppermute | solution.py:46
  171.5 38.4 %collective-permute-start.35 = (bf16[288,1024]{1,0:T(8,128)(2,1)S(1)}, bf16[288,1024]{1,0:T(8,128)(2,1)S(1)}, u32[]{:S(2)}, u32[]{:S(2)}) collective-permute-start(bf16[288,1024]{1,0:T(8,128)(2,1)S(1)} %collective-permute-done.33.refs_1_), channel_id=1, source_target_pairs={{0,1},{1,2},{2,3},{3,0},{4,5},{5,6},{6,7},{7,4},{8,9},{9,10},{10,1... | collective-permute-start | bytes 1769480 | tf_op jit(solution)/shard_map/ppermute | solution.py:46
  184.5 34.8 %collective-permute-start.49 = (bf16[288,1024]{1,0:T(8,128)(2,1)S(1)}, bf16[288,1024]{1,0:T(8,128)(2,1)S(1)}, u32[]{:S(2)}, u32[]{:S(2)}) collective-permute-start(bf16[288,1024]{1,0:T(8,128)(2,1)S(1)} %collective-permute-done.48.refs_2_), channel_id=1, source_target_pairs={{0,3},{1,0},{2,1},{3,2},{4,7},{5,4},{6,5},{7,6},{8,11},{9,8},{10,9... | collective-permute-start | bytes 1769480 | tf_op jit(solution)/shard_map/ppermute | solution.py:46
  202.3 12.1 %collective-permute-start.60 = (bf16[432,384]{1,0:T(8,128)(2,1)S(1)}, bf16[432,384]{1,0:T(8,128)(2,1)S(1)}, u32[]{:S(2)}, u32[]{:S(2)}) collective-permute-start(bf16[432,384]{1,0:T(8,128)(2,1)S(1)} %up0.1.refs_0_), channel_id=1, source_target_pairs={{0,3},{1,0},{2,1},{3,2},{4,7},{5,4},{6,5},{7,6},{8,11},{9,8},{10,9... | collective-permute-start | bytes 995336 | tf_op jit(solution)/shard_map/ppermute | solution.py:46
  202.3 17.0 %collective-permute-start.59 = (bf16[432,384]{1,0:T(8,128)(2,1)S(1)}, bf16[432,384]{1,0:T(8,128)(2,1)S(1)}, u32[]{:S(2)}, u32[]{:S(2)}) collective-permute-start(bf16[432,384]{1,0:T(8,128)(2,1)S(1)} %up0.1.refs_0_), channel_id=1, source_target_pairs={{0,1},{1,2},{2,3},{3,0},{4,5},{5,6},{6,7},{7,4},{8,9},{9,10},{10,1... | collective-permute-start | bytes 995336 | tf_op jit(solution)/shard_map/ppermute | solution.py:46
  205.5 18.8 %collective-permute-start.56 = (bf16[144,384]{1,0:T(8,128)(2,1)S(1)}, bf16[144,384]{1,0:T(8,128)(2,1)S(1)}, u32[]{:S(2)}, u32[]{:S(2)}) collective-permute-start(bf16[144,384]{1,0:T(8,128)(2,1)S(1)} %up1.1.refs_0_), channel_id=1, source_target_pairs={{0,3},{1,0},{2,1},{3,2},{4,7},{5,4},{6,5},{7,6},{8,11},{9,8},{10,9... | collective-permute-start | bytes 331784 | tf_op jit(solution)/shard_map/ppermute | solution.py:46
  209.9 15.9 %collective-permute-start.55 = (bf16[144,384]{1,0:T(8,128)(2,1)S(1)}, bf16[144,384]{1,0:T(8,128)(2,1)S(1)}, u32[]{:S(2)}, u32[]{:S(2)}) collective-permute-start(bf16[144,384]{1,0:T(8,128)(2,1)S(1)} %up1.1.refs_0_), channel_id=1, source_target_pairs={{0,1},{1,2},{2,3},{3,0},{4,5},{5,6},{6,7},{7,4},{8,9},{9,10},{10,1... | collective-permute-start | bytes 331784 | tf_op jit(solution)/shard_map/ppermute | solution.py:46
  214.4 12.3 %collective-permute-start.37 = (bf16[288,384]{1,0:T(8,128)(2,1)S(1)}, bf16[288,384]{1,0:T(8,128)(2,1)S(1)}, u32[]{:S(2)}, u32[]{:S(2)}) collective-permute-start(bf16[288,384]{1,0:T(8,128)(2,1)S(1)} %up3.1.refs_0_), channel_id=1, source_target_pairs={{0,3},{1,0},{2,1},{3,2},{4,7},{5,4},{6,5},{7,6},{8,11},{9,8},{10,9... | collective-permute-start | bytes 663560 | tf_op jit(solution)/shard_map/ppermute | solution.py:46
  219.3 19.5 %collective-permute-start.61 = (bf16[432,384]{1,0:T(8,128)(2,1)S(1)}, bf16[432,384]{1,0:T(8,128)(2,1)S(1)}, u32[]{:S(2)}, u32[]{:S(2)}) collective-permute-start(bf16[432,384]{1,0:T(8,128)(2,1)S(1)} %collective-permute-done.59.refs_1_), channel_id=1, source_target_pairs={{0,1},{1,2},{2,3},{3,0},{4,5},{5,6},{6,7},{7,4},{8,9},{9,10},{10,1... | collective-permute-start | bytes 995336 | tf_op jit(solution)/shard_map/ppermute | solution.py:46
  225.8 12.3 %collective-permute-start.50 = (bf16[288,384]{1,0:T(8,128)(2,1)S(1)}, bf16[288,384]{1,0:T(8,128)(2,1)S(1)}, u32[]{:S(2)}, u32[]{:S(2)}) collective-permute-start(bf16[288,384]{1,0:T(8,128)(2,1)S(1)} %up2.1.refs_0_), channel_id=1, source_target_pairs={{0,1},{1,2},{2,3},{3,0},{4,5},{5,6},{6,7},{7,4},{8,9},{9,10},{10,1... | collective-permute-start | bytes 663560 | tf_op jit(solution)/shard_map/ppermute | solution.py:46
  226.7 16.7 %collective-permute-start.57 = (bf16[144,384]{1,0:T(8,128)(2,1)S(1)}, bf16[144,384]{1,0:T(8,128)(2,1)S(1)}, u32[]{:S(2)}, u32[]{:S(2)}) collective-permute-start(bf16[144,384]{1,0:T(8,128)(2,1)S(1)} %collective-permute-done.56.refs_2_), channel_id=1, source_target_pairs={{0,3},{1,0},{2,1},{3,2},{4,7},{5,4},{6,5},{7,6},{8,11},{9,8},{10,9... | collective-permute-start | bytes 331784 | tf_op jit(solution)/shard_map/ppermute | solution.py:46
  228.5 24.8 %collective-permute-start.38 = (bf16[288,384]{1,0:T(8,128)(2,1)S(1)}, bf16[288,384]{1,0:T(8,128)(2,1)S(1)}, u32[]{:S(2)}, u32[]{:S(2)}) collective-permute-start(bf16[288,384]{1,0:T(8,128)(2,1)S(1)} %collective-permute-done.36.refs_1_), channel_id=1, source_target_pairs={{0,1},{1,2},{2,3},{3,0},{4,5},{5,6},{6,7},{7,4},{8,9},{9,10},{10,1... | collective-permute-start | bytes 663560 | tf_op jit(solution)/shard_map/ppermute | solution.py:46
  241.9 13.9 %collective-permute-start.62 = (bf16[144,1024]{1,0:T(8,128)(2,1)S(1)}, bf16[144,1024]{1,0:T(8,128)(2,1)S(1)}, u32[]{:S(2)}, u32[]{:S(2)}) collective-permute-start(bf16[144,1024]{1,0:T(8,128)(2,1)S(1)} %get-tuple-element.197), channel_id=1, source_target_pairs={{0,224},{32,0},{64,32},{96,64},{128,96},{160,128},{192,160},{224,1... | collective-permute-start | bytes 884744 | tf_op jit(solution)/shard_map/ppermute | solution.py:46
  242.0 17.4 %collective-permute-start.63 = (bf16[144,1024]{1,0:T(8,128)(2,1)S(1)}, bf16[144,1024]{1,0:T(8,128)(2,1)S(1)}, u32[]{:S(2)}, u32[]{:S(2)}) collective-permute-start(bf16[144,1024]{1,0:T(8,128)(2,1)S(1)} %get-tuple-element.198), channel_id=1, source_target_pairs={{0,32},{32,64},{64,96},{96,128},{128,160},{160,192},{192,224},{224... | collective-permute-start | bytes 884744 | tf_op jit(solution)/shard_map/ppermute | solution.py:46
  245.3 16.2 %collective-permute-start.58 = (bf16[144,1024]{1,0:T(8,128)(2,1)S(1)}, bf16[144,1024]{1,0:T(8,128)(2,1)S(1)}, u32[]{:S(2)}, u32[]{:S(2)}) collective-permute-start(bf16[144,1024]{1,0:T(8,128)(2,1)S(1)} %down1.1), channel_id=1, source_target_pairs={{0,128},{32,160},{64,192},{96,224},{128,0},{160,32},{192,64},{224,... | collective-permute-start | bytes 884744 | tf_op jit(solution)/shard_map/ppermute | solution.py:46
  248.7 20.7 %collective-permute-start.53 = (bf16[144,1024]{1,0:T(8,128)(2,1)S(1)}, bf16[144,1024]{1,0:T(8,128)(2,1)S(1)}, u32[]{:S(2)}, u32[]{:S(2)}) collective-permute-start(bf16[144,1024]{1,0:T(8,128)(2,1)S(1)} %get-tuple-element.186), channel_id=1, source_target_pairs={{0,160},{32,192},{64,224},{96,0},{128,32},{160,64},{192,96},{224,1... | collective-permute-start | bytes 884744 | tf_op jit(solution)/shard_map/ppermute | solution.py:46
  253.3 19.1 %collective-permute-start.54 = (bf16[144,1024]{1,0:T(8,128)(2,1)S(1)}, bf16[144,1024]{1,0:T(8,128)(2,1)S(1)}, u32[]{:S(2)}, u32[]{:S(2)}) collective-permute-start(bf16[144,1024]{1,0:T(8,128)(2,1)S(1)} %get-tuple-element.187), channel_id=1, source_target_pairs={{0,96},{32,128},{64,160},{96,192},{128,224},{160,0},{192,32},{224,... | collective-permute-start | bytes 884744 | tf_op jit(solution)/shard_map/ppermute | solution.py:46
  255.7 35.7 %collective-permute-start.45 = (bf16[144,1024]{1,0:T(8,128)(2,1)S(1)}, bf16[144,1024]{1,0:T(8,128)(2,1)S(1)}, u32[]{:S(2)}, u32[]{:S(2)}) collective-permute-start(bf16[144,1024]{1,0:T(8,128)(2,1)S(1)} %get-tuple-element.178), channel_id=1, source_target_pairs={{0,192},{32,224},{64,0},{96,32},{128,64},{160,96},{192,128},{224,1... | collective-permute-start | bytes 884744 | tf_op jit(solution)/shard_map/ppermute | solution.py:46
  259.3 32.1 %collective-permute-start.46 = (bf16[144,1024]{1,0:T(8,128)(2,1)S(1)}, bf16[144,1024]{1,0:T(8,128)(2,1)S(1)}, u32[]{:S(2)}, u32[]{:S(2)}) collective-permute-start(bf16[144,1024]{1,0:T(8,128)(2,1)S(1)} %get-tuple-element.179), channel_id=1, source_target_pairs={{0,64},{32,96},{64,128},{96,160},{128,192},{160,224},{192,0},{224,... | collective-permute-start | bytes 884744 | tf_op jit(solution)/shard_map/ppermute | solution.py:46
  292.5 9.7 %collective-permute-start.64 = (bf16[4,128,1024]{2,1,0:T(8,128)(2,1)S(1)}, bf16[4,128,1024]{2,1,0:T(8,128)(2,1)S(1)}, u32[]{:S(2)}, u32[]{:S(2)}) collective-permute-start(bf16[4,128,1024]{2,1,0:T(8,128)(2,1)S(1)} %combine3_4.1), channel_id=1, source_target_pairs={{0,4},{4,0},{1,5},{5,1},{2,6},{6,2},{3,7},{7,3},{8,12},{12,8},{9,1... | collective-permute-start | bytes 3145736 | tf_op jit(solution)/shard_map/ppermute | solution.py:46
  302.4 14.4 %collective-permute-start.65 = (bf16[128,1024]{1,0:T(8,128)(2,1)S(1)}, bf16[128,1024]{1,0:T(8,128)(2,1)S(1)}, u32[]{:S(2)}, u32[]{:S(2)}) collective-permute-start(bf16[128,1024]{1,0:T(8,128)(2,1)S(1)} %get-tuple-element.200), channel_id=1, source_target_pairs={{0,8},{8,16},{16,24},{24,0},{1,9},{9,17},{17,25},{25,1},{2,10},{10... | collective-permute-start | bytes 786440 | tf_op jit(solution)/shard_map/ppermute | solution.py:46
  302.4 14.3 %collective-permute-start.66 = (bf16[128,1024]{1,0:T(8,128)(2,1)S(1)}, bf16[128,1024]{1,0:T(8,128)(2,1)S(1)}, u32[]{:S(2)}, u32[]{:S(2)}) collective-permute-start(bf16[128,1024]{1,0:T(8,128)(2,1)S(1)} %get-tuple-element.201), channel_id=1, source_target_pairs={{0,24},{8,0},{16,8},{24,16},{1,25},{9,1},{17,9},{25,17},{2,26},{10... | collective-permute-start | bytes 786440 | tf_op jit(solution)/shard_map/ppermute | solution.py:46
  305.1 11.7 %collective-permute-start.67 = (bf16[128,1024]{1,0:T(8,128)(2,1)S(1)}, bf16[128,1024]{1,0:T(8,128)(2,1)S(1)}, u32[]{:S(2)}, u32[]{:S(2)}) collective-permute-start(bf16[128,1024]{1,0:T(8,128)(2,1)S(1)} %get-tuple-element.202), channel_id=1, source_target_pairs={{0,16},{8,24},{16,0},{24,8},{1,17},{9,25},{17,1},{25,9},{2,18},{10... | collective-permute-start | bytes 786440 | tf_op jit(solution)/shard_map/ppermute | solution.py:46
  (27 other events, 411.6 us)
where the time goes:
time: 322 us; the launch traced here: 318 us
  waiting for transfers between devices  151 us (47%)
  starting transfers between devices  123 us (38%)
  Pallas kernels  38.8 us (12%)
  local copies, waits for them, and re-layouts  4.32 us (1%)
    ppermute x68, waiting for transfers between devices, shift(): lax.ppermute(value, axis, [(i, (i + step) % count) for i in range(count)])  151 us
    ppermute x68, starting transfers between devices, shift(): lax.ppermute(value, axis, [(i, (i + step) % count) for i in range(count)])  123 us
    pallas_call x25, Pallas kernels, call(): pl.pallas_call(kernel, out_shape=outs, scratch_shapes=scratch, **blocks,...  38.8 us
  transfers between devices with their start and end apart: 68, of which 32 were waited for; matrix products, arithmetic and copies ran while one was open for 1% of the time, Pallas kernels for 10%

commit v1 on v0

--- a/solution.py
+++ b/solution.py
@@ -375,6 +375,8 @@
             at, right, left, far = rings[i - 2]
             *rows, far = lax.optimization_barrier((*rows, far))
             rings[i - 2] = at, right, left, far
+        if i == 1:
+            *rows, downs[3] = lax.optimization_barrier((*rows, downs[3]))
         count = len(group) * slots
         got.append(rows[0] if len(rows) == 1 else call(join_kernel, f"join{i}", shape(count, share), *rows, mib=8))
         if i > 0:
@@ -394,7 +396,6 @@
                 flops=4 * count * width * units,
             )
         )
-    acts[0], downs[3] = lax.optimization_barrier((acts[0], downs[3]))
     total = None
     for i, group in enumerate(GROUPS):
         count = got[i].shape[0]

time: 322 us -> 320 us (level)
  starting transfers between devices: 123 us -> 104 us
  waiting for transfers between devices: 151 us -> 168 us
    ppermute x68, starting transfers between devices: 123 us -> 104 us  [shift(): lax.ppermute(value, axis, [(i, (i + step) % count) for i in range(count)])]
    ppermute x68, waiting for transfers between devices: 151 us -> 168 us  [shift(): lax.ppermute(value, axis, [(i, (i + step) % count) for i in range(count)])]
  transfers between devices with their start and end apart: 68 -> 68, of which waited for: 32 -> 30; matrix products, arithmetic and copies ran while one was open for 1% -> 1% of each run, Pallas kernels for 10% -> 10%
where the time goes in v1:
time: 320 us; the launch traced here: 316 us
  waiting for transfers between devices  168 us (52%)
  starting transfers between devices  104 us (32%)
  Pallas kernels  38.8 us (12%)
  local copies, waits for them, and re-layouts  4.32 us (1%)
    ppermute x68, waiting for transfers between devices, shift(): lax.ppermute(value, axis, [(i, (i + step) % count) for i in range(count)])  168 us
    ppermute x68, starting transfers between devices, shift(): lax.ppermute(value, axis, [(i, (i + step) % count) for i in range(count)])  104 us
    pallas_call x25, Pallas kernels, call(): pl.pallas_call(kernel, out_shape=outs, scratch_shapes=scratch, **blocks,...  38.8 us
  transfers between devices with their start and end apart: 68, of which 30 were waited for; matrix products, arithmetic and copies ran while one was open for 1% of the time, Pallas kernels for 10%

profile of v1, /device:TPU:1, one launch (start us, length us, event | category | flops | bytes accessed | tf_op | source)
XLA Modules:
  0.0 315.9 jit_solution(6846753498917873023)
XLA Ops:
  0.0 6.4 %collective-permute-start.1 = (bf16[64,1024]{1,0:T(8,128)(2,1)}, bf16[64,1024]{1,0:T(8,128)(2,1)S(1)}, u32[]{:S(2)}, u32[]{:S(2)}) collective-permute-start(bf16[64,1024]{1,0:T(8,128)(2,1)} %bitcast.18), channel_id=1, source_target_pairs={{0,224},{32,0},{64,32},{96,64},{128,96},{160,128},{192,160},{224,1... | collective-permute-start | bytes 393224 | tf_op jit(solution)/shard_map/ppermute | solution.py:46
  7.7 2.6 collective-permute-start.10
  13.0 2.8 collective-permute-start.3
  17.7 3.1 collective-permute-start.5
  22.8 3.2 %collective-permute-start.7 = (bf16[32,1024]{1,0:T(8,128)(2,1)S(1)}, bf16[32,1024]{1,0:T(8,128)(2,1)S(1)}, u32[]{:S(2)}, u32[]{:S(2)}) collective-permute-start(bf16[32,1024]{1,0:T(8,128)(2,1)S(1)} %slice.9), channel_id=1, source_target_pairs={{0,224},{32,0},{64,32},{96,64},{128,96},{160,128},{192,160},{224,1... | collective-permute-start | bytes 196616 | tf_op jit(solution)/shard_map/ppermute | solution.py:46
  26.2 4.3 %collective-permute-done.6 = bf16[32,1024]{1,0:T(8,128)(2,1)S(1)} collective-permute-done((bf16[32,1024]{1,0:T(8,128)(2,1)S(1)}, bf16[32,1024]{1,0:T(8,128)(2,1)S(1)}, u32[]{:S(2)}, u32[]{:S(2)}) %collective-permute-start.6) | collective-permute-done | bytes 65568 | tf_op jit(solution)/shard_map/ppermute | solution.py:46
  30.6 5.7 %collective-permute-start.11 = (bf16[512,1024]{1,0:T(8,128)(2,1)S(1)}, bf16[512,1024]{1,0:T(8,128)(2,1)S(1)}, u32[]{:S(2)}, u32[]{:S(2)}) collective-permute-start(bf16[512,1024]{1,0:T(8,128)(2,1)S(1)} %constant_dynamic-update-slice_fusion.refs_4_), channel_id=1, source_target_pairs={{0,4},{4,0},{1,5},{5,1},{2,6},{6,2},{3,7},{7,3},{8,12},{12,8},{9,1... | collective-permute-start | bytes 3145736 | tf_op jit(solution)/shard_map/ppermute | solution.py:46
  39.1 2.9 project.1
  47.0 2.3 collective-permute-start.13
  51.4 5.1 %collective-permute-done.14.refs_3_.refs_7_ = bf16[160,256]{1,0:T(8,128)(2,1)S(1)} collective-permute-done((bf16[160,256]{1,0:T(8,128)(2,1)S(1)}, bf16[160,256]{1,0:T(8,128)(2,1)S(1)}, u32[]{:S(2)}, u32[]{:S(2)}) %collective-permute-start.14) | collective-permute-done | bytes 81952 | tf_op jit(solution)/shard_map/ppermute | solution.py:46
  56.5 2.6 collective-permute-start.18
  60.3 2.4 collective-permute-start.23
  64.5 6.9 %collective-permute-done.21.refs_3_ = bf16[512,256]{1,0:T(8,128)(2,1)S(1)} collective-permute-done((bf16[512,256]{1,0:T(8,128)(2,1)S(1)}, bf16[512,256]{1,0:T(8,128)(2,1)S(1)}, u32[]{:S(2)}, u32[]{:S(2)}) %collective-permute-start.21) | collective-permute-done | bytes 262176 | tf_op jit(solution)/shard_map/ppermute | solution.py:46
  71.4 2.9 collective-permute-done.20.refs_2_
  74.2 4.0 %collective-permute-done.19.refs_1_ = bf16[512,256]{1,0:T(8,128)(2,1)S(1)} collective-permute-done((bf16[512,256]{1,0:T(8,128)(2,1)S(1)}, bf16[512,256]{1,0:T(8,128)(2,1)S(1)}, u32[]{:S(2)}, u32[]{:S(2)}) %collective-permute-start.19) | collective-permute-done | bytes 262176 | tf_op jit(solution)/shard_map/ppermute | solution.py:46
  81.6 2.3 collective-permute-done.24.refs_6_
  83.9 2.6 dispatch.1
  86.6 2.7 collective-permute-start.26
  89.3 6.8 %collective-permute-done.25.refs_1_ = bf16[144,1024]{1,0:T(8,128)(2,1)S(1)} collective-permute-done((bf16[144,1024]{1,0:T(8,128)(2,1)S(1)}, bf16[144,1024]{1,0:T(8,128)(2,1)S(1)}, u32[]{:S(2)}, u32[]{:S(2)}) %collective-permute-start.25) | collective-permute-done | bytes 294944 | tf_op jit(solution)/shard_map/ppermute | solution.py:46
  96.1 11.7 %collective-permute-start.43 = (bf16[432,1024]{1,0:T(8,128)(2,1)S(1)}, bf16[432,1024]{1,0:T(8,128)(2,1)S(1)}, u32[]{:S(2)}, u32[]{:S(2)}) collective-permute-start(bf16[432,1024]{1,0:T(8,128)(2,1)S(1)} %join0.1.refs_0_), channel_id=1, source_target_pairs={{0,3},{1,0},{2,1},{3,2},{4,7},{5,4},{6,5},{7,6},{8,11},{9,8},{10,9... | collective-permute-start | bytes 2654216 | tf_op jit(solution)/shard_map/ppermute | solution.py:46
  110.3 34.2 %collective-permute-done.28.refs_7_ = bf16[384,1024]{1,0:T(8,128)(2,1)S(1)} collective-permute-done((bf16[384,1024]{1,0:T(8,128)(2,1)S(1)}, bf16[384,1024]{1,0:T(8,128)(2,1)S(1)}, u32[]{:S(2)}, u32[]{:S(2)}) %collective-permute-start.28) | collective-permute-done | bytes 786464 | tf_op jit(solution)/shard_map/ppermute | solution.py:46
  146.0 4.8 %collective-permute-done.30.refs_2_ = bf16[144,1024]{1,0:T(8,128)(2,1)S(1)} collective-permute-done((bf16[144,1024]{1,0:T(8,128)(2,1)S(1)}, bf16[144,1024]{1,0:T(8,128)(2,1)S(1)}, u32[]{:S(2)}, u32[]{:S(2)}) %collective-permute-start.30) | collective-permute-done | bytes 294944 | tf_op jit(solution)/shard_map/ppermute | solution.py:46
  151.8 3.6 %collective-permute-start.32 = (bf16[144,1024]{1,0:T(8,128)(2,1)S(1)}, bf16[144,1024]{1,0:T(8,128)(2,1)S(1)}, u32[]{:S(2)}, u32[]{:S(2)}) collective-permute-start(bf16[144,1024]{1,0:T(8,128)(2,1)S(1)} %get-tuple-element.157), channel_id=1, source_target_pairs={{0,192},{32,224},{64,0},{96,32},{128,64},{160,96},{192,128},{224,1... | collective-permute-start | bytes 884744 | tf_op jit(solution)/shard_map/ppermute | solution.py:46
  156.0 5.9 %collective-permute-done.31.refs_0_ = bf16[144,1024]{1,0:T(8,128)(2,1)S(1)} collective-permute-done((bf16[144,1024]{1,0:T(8,128)(2,1)S(1)}, bf16[144,1024]{1,0:T(8,128)(2,1)S(1)}, u32[]{:S(2)}, u32[]{:S(2)}) %collective-permute-start.31) | collective-permute-done | bytes 294944 | tf_op jit(solution)/shard_map/ppermute | solution.py:46
  161.9 4.6 %collective-permute-start.45 = (bf16[144,1024]{1,0:T(8,128)(2,1)S(1)}, bf16[144,1024]{1,0:T(8,128)(2,1)S(1)}, u32[]{:S(2)}, u32[]{:S(2)}) collective-permute-start(bf16[144,1024]{1,0:T(8,128)(2,1)S(1)} %get-tuple-element.177), channel_id=1, source_target_pairs={{0,160},{32,192},{64,224},{96,0},{128,32},{160,64},{192,96},{224,1... | collective-permute-start | bytes 884744 | tf_op jit(solution)/shard_map/ppermute | solution.py:46
  168.1 14.5 %collective-permute-done.44.refs_0_ = bf16[144,1024]{1,0:T(8,128)(2,1)S(1)} collective-permute-done((bf16[144,1024]{1,0:T(8,128)(2,1)S(1)}, bf16[144,1024]{1,0:T(8,128)(2,1)S(1)}, u32[]{:S(2)}, u32[]{:S(2)}) %collective-permute-start.44) | collective-permute-done | bytes 294944 | tf_op jit(solution)/shard_map/ppermute | solution.py:46
  182.7 3.6 %collective-permute-start.48 = (bf16[288,1024]{1,0:T(8,128)(2,1)S(1)}, bf16[288,1024]{1,0:T(8,128)(2,1)S(1)}, u32[]{:S(2)}, u32[]{:S(2)}) collective-permute-start(bf16[288,1024]{1,0:T(8,128)(2,1)S(1)} %join2.1.refs_0_), channel_id=1, source_target_pairs={{0,3},{1,0},{2,1},{3,2},{4,7},{5,4},{6,5},{7,6},{8,11},{9,8},{10,9... | collective-permute-start | bytes 1769480 | tf_op jit(solution)/shard_map/ppermute | solution.py:46
  186.4 12.1 %collective-permute-done.48.refs_2_ = bf16[288,1024]{1,0:T(8,128)(2,1)S(1)} collective-permute-done((bf16[288,1024]{1,0:T(8,128)(2,1)S(1)}, bf16[288,1024]{1,0:T(8,128)(2,1)S(1)}, u32[]{:S(2)}, u32[]{:S(2)}) %collective-permute-start.48) | collective-permute-done | bytes 589856 | tf_op jit(solution)/shard_map/ppermute | solution.py:46
  198.4 3.7 %collective-permute-done.47.refs_1_ = bf16[288,1024]{1,0:T(8,128)(2,1)S(1)} collective-permute-done((bf16[288,1024]{1,0:T(8,128)(2,1)S(1)}, bf16[288,1024]{1,0:T(8,128)(2,1)S(1)}, u32[]{:S(2)}, u32[]{:S(2)}) %collective-permute-start.47) | collective-permute-done | bytes 589856 | tf_op jit(solution)/shard_map/ppermute | solution.py:46
  202.6 4.6 %up0.1.refs_0_ = bf16[432,384]{1,0:T(8,128)(2,1)S(1)} custom-call(bf16[432,1024]{1,0:T(8,128)(2,1)S(1)} %join0.1.refs_0_, bf16[432,1024]{1,0:T(8,128)(2,1)S(1)} %collective-permute-done.42.refs_1_, bf16[432,1024]{1,0:T(8,128)(2,1)S(1)} %collective-permute-done.43.refs_2_, bf16[432,1024]{1,0:T(8,128)(2,1)S(1)} %collective-permute-done.46.refs_3_, ...), custom_call_target="tpu_custom_call" | custom-call | flops 2717908992 | bytes 9846784 | tf_op jit(solution)/shard_map/up0/pallas_call | solution.py:32
  211.9 2.9 collective-permute-done.36.refs_3_
  214.8 3.2 %up3.1.refs_0_ = bf16[288,384]{1,0:T(8,128)(2,1)S(1)} custom-call(bf16[288,1024]{1,0:T(8,128)(2,1)S(1)} %join3.1.refs_0_, bf16[288,1024]{1,0:T(8,128)(2,1)S(1)} %collective-permute-done.34.refs_1_, bf16[288,1024]{1,0:T(8,128)(2,1)S(1)} %collective-permute-done.35.refs_2_, bf16[288,1024]{1,0:T(8,128)(2,1)S(1)} %collective-permute-done.36.refs_3_, ...), custom_call_target="tpu_custom_call" | custom-call | flops 1811939328 | bytes 8667136 | tf_op jit(solution)/shard_map/up3/pallas_call | solution.py:32
  218.0 2.7 collective-permute-start.38
  222.1 3.2 %up2.1.refs_0_ = bf16[288,384]{1,0:T(8,128)(2,1)S(1)} custom-call(bf16[288,1024]{1,0:T(8,128)(2,1)S(1)} %join2.1.refs_0_, bf16[288,1024]{1,0:T(8,128)(2,1)S(1)} %collective-permute-done.47.refs_1_, bf16[288,1024]{1,0:T(8,128)(2,1)S(1)} %collective-permute-done.48.refs_2_, bf16[288,1024]{1,0:T(8,128)(2,1)S(1)} %collective-permute-done.49.refs_3_, ...), custom_call_target="tpu_custom_call" | custom-call | flops 1811939328 | bytes 8667136 | tf_op jit(solution)/shard_map/up2/pallas_call | solution.py:32
  225.3 2.7 collective-permute-start.51
  228.0 2.7 collective-permute-start.57
  231.8 5.0 %collective-permute-done.50.refs_1_ = bf16[288,384]{1,0:T(8,128)(2,1)S(1)} collective-permute-done((bf16[288,384]{1,0:T(8,128)(2,1)S(1)}, bf16[288,384]{1,0:T(8,128)(2,1)S(1)}, u32[]{:S(2)}, u32[]{:S(2)}) %collective-permute-start.50) | collective-permute-done | bytes 221216 | tf_op jit(solution)/shard_map/ppermute | solution.py:46
  236.8 3.1 down0.1
  244.1 2.5 down2.1
  246.5 3.5 %collective-permute-start.53 = (bf16[144,1024]{1,0:T(8,128)(2,1)S(1)}, bf16[144,1024]{1,0:T(8,128)(2,1)S(1)}, u32[]{:S(2)}, u32[]{:S(2)}) collective-permute-start(bf16[144,1024]{1,0:T(8,128)(2,1)S(1)} %get-tuple-element.184), channel_id=1, source_target_pairs={{0,160},{32,192},{64,224},{96,0},{128,32},{160,64},{192,96},{224,1... | collective-permute-start | bytes 884744 | tf_op jit(solution)/shard_map/ppermute | solution.py:46
  250.3 2.5 down3.1
  252.7 2.6 collective-permute-start.40
  259.8 7.4 %collective-permute-done.53.refs_0_ = bf16[144,1024]{1,0:T(8,128)(2,1)S(1)} collective-permute-done((bf16[144,1024]{1,0:T(8,128)(2,1)S(1)}, bf16[144,1024]{1,0:T(8,128)(2,1)S(1)}, u32[]{:S(2)}, u32[]{:S(2)}) %collective-permute-start.53) | collective-permute-done | bytes 294944 | tf_op jit(solution)/shard_map/ppermute | solution.py:46
  267.1 3.3 %collective-permute-done.54.refs_1_ = bf16[144,1024]{1,0:T(8,128)(2,1)S(1)} collective-permute-done((bf16[144,1024]{1,0:T(8,128)(2,1)S(1)}, bf16[144,1024]{1,0:T(8,128)(2,1)S(1)}, u32[]{:S(2)}, u32[]{:S(2)}) %collective-permute-start.54) | collective-permute-done | bytes 294944 | tf_op jit(solution)/shard_map/ppermute | solution.py:46
  272.5 17.8 %collective-permute-done.40.refs_0_ = bf16[144,1024]{1,0:T(8,128)(2,1)S(1)} collective-permute-done((bf16[144,1024]{1,0:T(8,128)(2,1)S(1)}, bf16[144,1024]{1,0:T(8,128)(2,1)S(1)}, u32[]{:S(2)}, u32[]{:S(2)}) %collective-permute-start.40) | collective-permute-done | bytes 294944 | tf_op jit(solution)/shard_map/ppermute | solution.py:46
  291.4 6.5 %collective-permute-start.64 = (bf16[4,128,1024]{2,1,0:T(8,128)(2,1)S(1)}, bf16[4,128,1024]{2,1,0:T(8,128)(2,1)S(1)}, u32[]{:S(2)}, u32[]{:S(2)}) collective-permute-start(bf16[4,128,1024]{2,1,0:T(8,128)(2,1)S(1)} %combine3_4.1), channel_id=1, source_target_pairs={{0,4},{4,0},{1,5},{5,1},{2,6},{6,2},{3,7},{7,3},{8,12},{12,8},{9,1... | collective-permute-start | bytes 3145736 | tf_op jit(solution)/shard_map/ppermute | solution.py:46
  300.5 2.7 collective-permute-start.66
  303.1 11.7 %collective-permute-done.65.refs_1_ = bf16[128,1024]{1,0:T(8,128)(2,1)S(1)} collective-permute-done((bf16[128,1024]{1,0:T(8,128)(2,1)S(1)}, bf16[128,1024]{1,0:T(8,128)(2,1)S(1)}, u32[]{:S(2)}, u32[]{:S(2)}) %collective-permute-start.65) | collective-permute-done | bytes 262176 | tf_op jit(solution)/shard_map/ppermute | solution.py:46
  (139 shorter events, 55.0 us)
Async XLA Ops:
  0.0 13.0 %collective-permute-start.1 = (bf16[64,1024]{1,0:T(8,128)(2,1)}, bf16[64,1024]{1,0:T(8,128)(2,1)S(1)}, u32[]{:S(2)}, u32[]{:S(2)}) collective-permute-start(bf16[64,1024]{1,0:T(8,128)(2,1)} %bitcast.18), channel_id=1, source_target_pairs={{0,224},{32,0},{64,32},{96,64},{128,96},{160,128},{192,160},{224,1... | collective-permute-start | bytes 393224 | tf_op jit(solution)/shard_map/ppermute | solution.py:46
  6.4 9.4 %collective-permute-start = (bf16[64,1024]{1,0:T(8,128)(2,1)}, bf16[64,1024]{1,0:T(8,128)(2,1)S(1)}, u32[]{:S(2)}, u32[]{:S(2)}) collective-permute-start(bf16[64,1024]{1,0:T(8,128)(2,1)} %bitcast.19), channel_id=1, source_target_pairs={{0,32},{32,64},{64,96},{96,128},{128,160},{160,192},{192,224},{224... | collective-permute-start | bytes 393224 | tf_op jit(solution)/shard_map/ppermute | solution.py:46
  6.4 24.1 %collective-permute-start.8 = (bf16[128,1024]{1,0:T(8,128)(2,1)}, bf16[128,1024]{1,0:T(8,128)(2,1)S(1)}, u32[]{:S(2)}, u32[]{:S(2)}) collective-permute-start(bf16[128,1024]{1,0:T(8,128)(2,1)} %refs_0_), channel_id=1, source_target_pairs={{0,8},{8,16},{16,24},{24,0},{1,9},{9,17},{17,25},{25,1},{2,10},{10... | collective-permute-start | bytes 786440 | tf_op jit(solution)/shard_map/ppermute | solution.py:46
  7.7 22.8 %collective-permute-start.10 = (bf16[128,1024]{1,0:T(8,128)(2,1)}, bf16[128,1024]{1,0:T(8,128)(2,1)S(1)}, u32[]{:S(2)}, u32[]{:S(2)}) collective-permute-start(bf16[128,1024]{1,0:T(8,128)(2,1)} %refs_0_), channel_id=1, source_target_pairs={{0,16},{8,24},{16,0},{24,8},{1,17},{9,25},{17,1},{25,9},{2,18},{10... | collective-permute-start | bytes 786440 | tf_op jit(solution)/shard_map/ppermute | solution.py:46
  10.3 20.2 %collective-permute-start.9 = (bf16[128,1024]{1,0:T(8,128)(2,1)}, bf16[128,1024]{1,0:T(8,128)(2,1)S(1)}, u32[]{:S(2)}, u32[]{:S(2)}) collective-permute-start(bf16[128,1024]{1,0:T(8,128)(2,1)} %refs_0_), channel_id=1, source_target_pairs={{0,24},{8,0},{16,8},{24,16},{1,25},{9,1},{17,9},{25,17},{2,26},{10... | collective-permute-start | bytes 786440 | tf_op jit(solution)/shard_map/ppermute | solution.py:46
  42.1 17.9 %collective-permute-start.15 = (bf16[4,128,256]{2,1,0:T(8,128)(2,1)S(1)}, bf16[4,128,256]{2,1,0:T(8,128)(2,1)S(1)}, u32[]{:S(2)}, u32[]{:S(2)}) collective-permute-start(bf16[4,128,256]{2,1,0:T(8,128)(2,1)S(1)} %get-tuple-element.124), channel_id=1, source_target_pairs={{0,1},{1,2},{2,3},{3,0},{4,5},{5,6},{6,7},{7,4},{8,9},{9,10},{10,1... | collective-permute-start | bytes 786440 | tf_op jit(solution)/shard_map/ppermute | solution.py:46
  43.4 16.6 %collective-permute-start.16 = (bf16[4,128,256]{2,1,0:T(8,128)(2,1)S(1)}, bf16[4,128,256]{2,1,0:T(8,128)(2,1)S(1)}, u32[]{:S(2)}, u32[]{:S(2)}) collective-permute-start(bf16[4,128,256]{2,1,0:T(8,128)(2,1)S(1)} %get-tuple-element.125), channel_id=1, source_target_pairs={{0,3},{1,0},{2,1},{3,2},{4,7},{5,4},{6,5},{7,6},{8,11},{9,8},{10,9... | collective-permute-start | bytes 786440 | tf_op jit(solution)/shard_map/ppermute | solution.py:46
  44.8 15.1 %collective-permute-start.17 = (bf16[4,128,256]{2,1,0:T(8,128)(2,1)S(1)}, bf16[4,128,256]{2,1,0:T(8,128)(2,1)S(1)}, u32[]{:S(2)}, u32[]{:S(2)}) collective-permute-start(bf16[4,128,256]{2,1,0:T(8,128)(2,1)S(1)} %get-tuple-element.126), channel_id=1, source_target_pairs={{0,2},{1,3},{2,0},{3,1},{4,6},{5,7},{6,4},{7,5},{8,10},{9,11},{10,... | collective-permute-start | bytes 786440 | tf_op jit(solution)/shard_map/ppermute | solution.py:46
  59.9 20.1 %collective-permute-start.22 = (bf16[384,1024]{1,0:T(8,128)(2,1)S(1)}, bf16[384,1024]{1,0:T(8,128)(2,1)S(1)}, u32[]{:S(2)}, u32[]{:S(2)}) collective-permute-start(bf16[384,1024]{1,0:T(8,128)(2,1)S(1)} %get-tuple-element.137), channel_id=1, source_target_pairs={{0,1},{1,2},{2,3},{3,0},{4,5},{5,6},{6,7},{7,4},{8,9},{9,10},{10,1... | collective-permute-start | bytes 2359304 | tf_op jit(solution)/shard_map/ppermute | solution.py:46
  60.3 19.7 %collective-permute-start.23 = (bf16[384,1024]{1,0:T(8,128)(2,1)S(1)}, bf16[384,1024]{1,0:T(8,128)(2,1)S(1)}, u32[]{:S(2)}, u32[]{:S(2)}) collective-permute-start(bf16[384,1024]{1,0:T(8,128)(2,1)S(1)} %get-tuple-element.138), channel_id=1, source_target_pairs={{0,3},{1,0},{2,1},{3,2},{4,7},{5,4},{6,5},{7,6},{8,11},{9,8},{10,9... | collective-permute-start | bytes 2359304 | tf_op jit(solution)/shard_map/ppermute | solution.py:46
  62.9 11.3 %collective-permute-start.20 = (bf16[512,256]{1,0:T(8,128)(2,1)S(1)}, bf16[512,256]{1,0:T(8,128)(2,1)S(1)}, u32[]{:S(2)}, u32[]{:S(2)}) collective-permute-start(bf16[512,256]{1,0:T(8,128)(2,1)S(1)} %hidden.1.refs_0_), channel_id=1, source_target_pairs={{0,24},{8,0},{16,8},{24,16},{1,25},{9,1},{17,9},{25,17},{2,26},{10... | collective-permute-start | bytes 786440 | tf_op jit(solution)/shard_map/ppermute | solution.py:46
  64.5 13.8 %collective-permute-start.19 = (bf16[512,256]{1,0:T(8,128)(2,1)S(1)}, bf16[512,256]{1,0:T(8,128)(2,1)S(1)}, u32[]{:S(2)}, u32[]{:S(2)}) collective-permute-start(bf16[512,256]{1,0:T(8,128)(2,1)S(1)} %hidden.1.refs_0_), channel_id=1, source_target_pairs={{0,8},{8,16},{16,24},{24,0},{1,9},{9,17},{17,25},{25,1},{2,10},{10... | collective-permute-start | bytes 786440 | tf_op jit(solution)/shard_map/ppermute | solution.py:46
  86.5 9.5 %collective-permute-start.25 = (bf16[144,1024]{1,0:T(8,128)(2,1)S(1)}, bf16[144,1024]{1,0:T(8,128)(2,1)S(1)}, u32[]{:S(2)}, u32[]{:S(2)}) collective-permute-start(bf16[144,1024]{1,0:T(8,128)(2,1)S(1)} %get-tuple-element.149), channel_id=1, source_target_pairs={{0,32},{32,64},{64,96},{96,128},{128,160},{160,192},{192,224},{224... | collective-permute-start | bytes 884744 | tf_op jit(solution)/shard_map/ppermute | solution.py:46
  86.6 9.4 %collective-permute-start.26 = (bf16[144,1024]{1,0:T(8,128)(2,1)S(1)}, bf16[144,1024]{1,0:T(8,128)(2,1)S(1)}, u32[]{:S(2)}, u32[]{:S(2)}) collective-permute-start(bf16[144,1024]{1,0:T(8,128)(2,1)S(1)} %get-tuple-element.150), channel_id=1, source_target_pairs={{0,224},{32,0},{64,32},{96,64},{128,96},{160,128},{192,160},{224,1... | collective-permute-start | bytes 884744 | tf_op jit(solution)/shard_map/ppermute | solution.py:46
  96.1 49.8 %collective-permute-start.43 = (bf16[432,1024]{1,0:T(8,128)(2,1)S(1)}, bf16[432,1024]{1,0:T(8,128)(2,1)S(1)}, u32[]{:S(2)}, u32[]{:S(2)}) collective-permute-start(bf16[432,1024]{1,0:T(8,128)(2,1)S(1)} %join0.1.refs_0_), channel_id=1, source_target_pairs={{0,3},{1,0},{2,1},{3,2},{4,7},{5,4},{6,5},{7,6},{8,11},{9,8},{10,9... | collective-permute-start | bytes 2654216 | tf_op jit(solution)/shard_map/ppermute | solution.py:46
  107.8 38.1 %collective-permute-start.42 = (bf16[432,1024]{1,0:T(8,128)(2,1)S(1)}, bf16[432,1024]{1,0:T(8,128)(2,1)S(1)}, u32[]{:S(2)}, u32[]{:S(2)}) collective-permute-start(bf16[432,1024]{1,0:T(8,128)(2,1)S(1)} %join0.1.refs_0_), channel_id=1, source_target_pairs={{0,1},{1,2},{2,3},{3,0},{4,5},{5,6},{6,7},{7,4},{8,9},{9,10},{10,1... | collective-permute-start | bytes 2654216 | tf_op jit(solution)/shard_map/ppermute | solution.py:46
  107.8 36.7 %collective-permute-start.28 = (bf16[384,1024]{1,0:T(8,128)(2,1)S(1)}, bf16[384,1024]{1,0:T(8,128)(2,1)S(1)}, u32[]{:S(2)}, u32[]{:S(2)}) collective-permute-start(bf16[384,1024]{1,0:T(8,128)(2,1)S(1)} %get-tuple-element.152), channel_id=1, source_target_pairs={{0,2},{1,3},{2,0},{3,1},{4,6},{5,7},{6,4},{7,5},{8,10},{9,11},{10,... | collective-permute-start | bytes 2359304 | tf_op jit(solution)/shard_map/ppermute | solution.py:46
  109.0 35.4 %collective-permute-start.27 = (bf16[144,1024]{1,0:T(8,128)(2,1)S(1)}, bf16[144,1024]{1,0:T(8,128)(2,1)S(1)}, u32[]{:S(2)}, u32[]{:S(2)}) collective-permute-start(bf16[144,1024]{1,0:T(8,128)(2,1)S(1)} %get-tuple-element.151), channel_id=1, source_target_pairs={{0,128},{32,160},{64,192},{96,224},{128,0},{160,32},{192,64},{224,... | collective-permute-start | bytes 884744 | tf_op jit(solution)/shard_map/ppermute | solution.py:46
  145.9 36.8 %collective-permute-start.46 = (bf16[432,1024]{1,0:T(8,128)(2,1)S(1)}, bf16[432,1024]{1,0:T(8,128)(2,1)S(1)}, u32[]{:S(2)}, u32[]{:S(2)}) collective-permute-start(bf16[432,1024]{1,0:T(8,128)(2,1)S(1)} %collective-permute-done.42.refs_1_), channel_id=1, source_target_pairs={{0,1},{1,2},{2,3},{3,0},{4,5},{5,6},{6,7},{7,4},{8,9},{9,10},{10,1... | collective-permute-start | bytes 2654216 | tf_op jit(solution)/shard_map/ppermute | solution.py:46
  151.8 10.1 %collective-permute-start.31 = (bf16[144,1024]{1,0:T(8,128)(2,1)S(1)}, bf16[144,1024]{1,0:T(8,128)(2,1)S(1)}, u32[]{:S(2)}, u32[]{:S(2)}) collective-permute-start(bf16[144,1024]{1,0:T(8,128)(2,1)S(1)} %get-tuple-element.156), channel_id=1, source_target_pairs={{0,64},{32,96},{64,128},{96,160},{128,192},{160,224},{192,0},{224,... | collective-permute-start | bytes 884744 | tf_op jit(solution)/shard_map/ppermute | solution.py:46
  151.8 14.8 %collective-permute-start.32 = (bf16[144,1024]{1,0:T(8,128)(2,1)S(1)}, bf16[144,1024]{1,0:T(8,128)(2,1)S(1)}, u32[]{:S(2)}, u32[]{:S(2)}) collective-permute-start(bf16[144,1024]{1,0:T(8,128)(2,1)S(1)} %get-tuple-element.157), channel_id=1, source_target_pairs={{0,192},{32,224},{64,0},{96,32},{128,64},{160,96},{192,128},{224,1... | collective-permute-start | bytes 884744 | tf_op jit(solution)/shard_map/ppermute | solution.py:46
  155.3 11.2 %collective-permute-start.33 = (bf16[144,1024]{1,0:T(8,128)(2,1)S(1)}, bf16[144,1024]{1,0:T(8,128)(2,1)S(1)}, u32[]{:S(2)}, u32[]{:S(2)}) collective-permute-start(bf16[144,1024]{1,0:T(8,128)(2,1)S(1)} %collective-permute-done.30.refs_2_), channel_id=1, source_target_pairs={{0,3},{1,0},{2,1},{3,2},{4,7},{5,4},{6,5},{7,6},{8,11},{9,8},{10,9... | collective-permute-start | bytes 884744 | tf_op jit(solution)/shard_map/ppermute | solution.py:46
  156.0 26.6 %collective-permute-start.44 = (bf16[144,1024]{1,0:T(8,128)(2,1)S(1)}, bf16[144,1024]{1,0:T(8,128)(2,1)S(1)}, u32[]{:S(2)}, u32[]{:S(2)}) collective-permute-start(bf16[144,1024]{1,0:T(8,128)(2,1)S(1)} %get-tuple-element.176), channel_id=1, source_target_pairs={{0,96},{32,128},{64,160},{96,192},{128,224},{160,0},{192,32},{224,... | collective-permute-start | bytes 884744 | tf_op jit(solution)/shard_map/ppermute | solution.py:46
  161.9 20.8 %collective-permute-start.45 = (bf16[144,1024]{1,0:T(8,128)(2,1)S(1)}, bf16[144,1024]{1,0:T(8,128)(2,1)S(1)}, u32[]{:S(2)}, u32[]{:S(2)}) collective-permute-start(bf16[144,1024]{1,0:T(8,128)(2,1)S(1)} %get-tuple-element.177), channel_id=1, source_target_pairs={{0,160},{32,192},{64,224},{96,0},{128,32},{160,64},{192,96},{224,1... | collective-permute-start | bytes 884744 | tf_op jit(solution)/shard_map/ppermute | solution.py:46
  166.6 19.7 %collective-permute-start.35 = (bf16[288,1024]{1,0:T(8,128)(2,1)S(1)}, bf16[288,1024]{1,0:T(8,128)(2,1)S(1)}, u32[]{:S(2)}, u32[]{:S(2)}) collective-permute-start(bf16[288,1024]{1,0:T(8,128)(2,1)S(1)} %join3.1.refs_0_), channel_id=1, source_target_pairs={{0,3},{1,0},{2,1},{3,2},{4,7},{5,4},{6,5},{7,6},{8,11},{9,8},{10,9... | collective-permute-start | bytes 1769480 | tf_op jit(solution)/shard_map/ppermute | solution.py:46
  166.7 19.6 %collective-permute-start.34 = (bf16[288,1024]{1,0:T(8,128)(2,1)S(1)}, bf16[288,1024]{1,0:T(8,128)(2,1)S(1)}, u32[]{:S(2)}, u32[]{:S(2)}) collective-permute-start(bf16[288,1024]{1,0:T(8,128)(2,1)S(1)} %join3.1.refs_0_), channel_id=1, source_target_pairs={{0,1},{1,2},{2,3},{3,0},{4,5},{5,6},{6,7},{7,4},{8,9},{9,10},{10,1... | collective-permute-start | bytes 1769480 | tf_op jit(solution)/shard_map/ppermute | solution.py:46
  182.7 15.7 %collective-permute-start.48 = (bf16[288,1024]{1,0:T(8,128)(2,1)S(1)}, bf16[288,1024]{1,0:T(8,128)(2,1)S(1)}, u32[]{:S(2)}, u32[]{:S(2)}) collective-permute-start(bf16[288,1024]{1,0:T(8,128)(2,1)S(1)} %join2.1.refs_0_), channel_id=1, source_target_pairs={{0,3},{1,0},{2,1},{3,2},{4,7},{5,4},{6,5},{7,6},{8,11},{9,8},{10,9... | collective-permute-start | bytes 1769480 | tf_op jit(solution)/shard_map/ppermute | solution.py:46
  186.3 15.9 %collective-permute-start.47 = (bf16[288,1024]{1,0:T(8,128)(2,1)S(1)}, bf16[288,1024]{1,0:T(8,128)(2,1)S(1)}, u32[]{:S(2)}, u32[]{:S(2)}) collective-permute-start(bf16[288,1024]{1,0:T(8,128)(2,1)S(1)} %join2.1.refs_0_), channel_id=1, source_target_pairs={{0,1},{1,2},{2,3},{3,0},{4,5},{5,6},{6,7},{7,4},{8,9},{9,10},{10,1... | collective-permute-start | bytes 1769480 | tf_op jit(solution)/shard_map/ppermute | solution.py:46
  186.3 28.5 %collective-permute-start.36 = (bf16[288,1024]{1,0:T(8,128)(2,1)S(1)}, bf16[288,1024]{1,0:T(8,128)(2,1)S(1)}, u32[]{:S(2)}, u32[]{:S(2)}) collective-permute-start(bf16[288,1024]{1,0:T(8,128)(2,1)S(1)} %collective-permute-done.34.refs_1_), channel_id=1, source_target_pairs={{0,1},{1,2},{2,3},{3,0},{4,5},{5,6},{6,7},{7,4},{8,9},{9,10},{10,1... | collective-permute-start | bytes 1769480 | tf_op jit(solution)/shard_map/ppermute | solution.py:46
  202.1 19.8 %collective-permute-start.49 = (bf16[288,1024]{1,0:T(8,128)(2,1)S(1)}, bf16[288,1024]{1,0:T(8,128)(2,1)S(1)}, u32[]{:S(2)}, u32[]{:S(2)}) collective-permute-start(bf16[288,1024]{1,0:T(8,128)(2,1)S(1)} %collective-permute-done.48.refs_2_), channel_id=1, source_target_pairs={{0,3},{1,0},{2,1},{3,2},{4,7},{5,4},{6,5},{7,6},{8,11},{9,8},{10,9... | collective-permute-start | bytes 1769480 | tf_op jit(solution)/shard_map/ppermute | solution.py:46
  207.2 10.8 %collective-permute-start.60 = (bf16[432,384]{1,0:T(8,128)(2,1)S(1)}, bf16[432,384]{1,0:T(8,128)(2,1)S(1)}, u32[]{:S(2)}, u32[]{:S(2)}) collective-permute-start(bf16[432,384]{1,0:T(8,128)(2,1)S(1)} %up0.1.refs_0_), channel_id=1, source_target_pairs={{0,3},{1,0},{2,1},{3,2},{4,7},{5,4},{6,5},{7,6},{8,11},{9,8},{10,9... | collective-permute-start | bytes 995336 | tf_op jit(solution)/shard_map/ppermute | solution.py:46
  207.3 14.6 %collective-permute-start.59 = (bf16[432,384]{1,0:T(8,128)(2,1)S(1)}, bf16[432,384]{1,0:T(8,128)(2,1)S(1)}, u32[]{:S(2)}, u32[]{:S(2)}) collective-permute-start(bf16[432,384]{1,0:T(8,128)(2,1)S(1)} %up0.1.refs_0_), channel_id=1, source_target_pairs={{0,1},{1,2},{2,3},{3,0},{4,5},{5,6},{6,7},{7,4},{8,9},{9,10},{10,1... | collective-permute-start | bytes 995336 | tf_op jit(solution)/shard_map/ppermute | solution.py:46
  210.5 14.7 %collective-permute-start.56 = (bf16[144,384]{1,0:T(8,128)(2,1)S(1)}, bf16[144,384]{1,0:T(8,128)(2,1)S(1)}, u32[]{:S(2)}, u32[]{:S(2)}) collective-permute-start(bf16[144,384]{1,0:T(8,128)(2,1)S(1)} %up1.1.refs_0_), channel_id=1, source_target_pairs={{0,3},{1,0},{2,1},{3,2},{4,7},{5,4},{6,5},{7,6},{8,11},{9,8},{10,9... | collective-permute-start | bytes 331784 | tf_op jit(solution)/shard_map/ppermute | solution.py:46
  214.8 13.2 %collective-permute-start.55 = (bf16[144,384]{1,0:T(8,128)(2,1)S(1)}, bf16[144,384]{1,0:T(8,128)(2,1)S(1)}, u32[]{:S(2)}, u32[]{:S(2)}) collective-permute-start(bf16[144,384]{1,0:T(8,128)(2,1)S(1)} %up1.1.refs_0_), channel_id=1, source_target_pairs={{0,1},{1,2},{2,3},{3,0},{4,5},{5,6},{6,7},{7,4},{8,9},{9,10},{10,1... | collective-permute-start | bytes 331784 | tf_op jit(solution)/shard_map/ppermute | solution.py:46
  218.0 10.0 %collective-permute-start.38 = (bf16[288,384]{1,0:T(8,128)(2,1)S(1)}, bf16[288,384]{1,0:T(8,128)(2,1)S(1)}, u32[]{:S(2)}, u32[]{:S(2)}) collective-permute-start(bf16[288,384]{1,0:T(8,128)(2,1)S(1)} %up3.1.refs_0_), channel_id=1, source_target_pairs={{0,3},{1,0},{2,1},{3,2},{4,7},{5,4},{6,5},{7,6},{8,11},{9,8},{10,9... | collective-permute-start | bytes 663560 | tf_op jit(solution)/shard_map/ppermute | solution.py:46
  221.9 14.9 %collective-permute-start.61 = (bf16[432,384]{1,0:T(8,128)(2,1)S(1)}, bf16[432,384]{1,0:T(8,128)(2,1)S(1)}, u32[]{:S(2)}, u32[]{:S(2)}) collective-permute-start(bf16[432,384]{1,0:T(8,128)(2,1)S(1)} %collective-permute-done.59.refs_1_), channel_id=1, source_target_pairs={{0,1},{1,2},{2,3},{3,0},{4,5},{5,6},{6,7},{7,4},{8,9},{9,10},{10,1... | collective-permute-start | bytes 995336 | tf_op jit(solution)/shard_map/ppermute | solution.py:46
  228.0 13.4 %collective-permute-start.57 = (bf16[144,384]{1,0:T(8,128)(2,1)S(1)}, bf16[144,384]{1,0:T(8,128)(2,1)S(1)}, u32[]{:S(2)}, u32[]{:S(2)}) collective-permute-start(bf16[144,384]{1,0:T(8,128)(2,1)S(1)} %collective-permute-done.56.refs_2_), channel_id=1, source_target_pairs={{0,3},{1,0},{2,1},{3,2},{4,7},{5,4},{6,5},{7,6},{8,11},{9,8},{10,9... | collective-permute-start | bytes 331784 | tf_op jit(solution)/shard_map/ppermute | solution.py:46
  230.7 19.4 %collective-permute-start.39 = (bf16[288,384]{1,0:T(8,128)(2,1)S(1)}, bf16[288,384]{1,0:T(8,128)(2,1)S(1)}, u32[]{:S(2)}, u32[]{:S(2)}) collective-permute-start(bf16[288,384]{1,0:T(8,128)(2,1)S(1)} %collective-permute-done.37.refs_1_), channel_id=1, source_target_pairs={{0,1},{1,2},{2,3},{3,0},{4,5},{5,6},{6,7},{7,4},{8,9},{9,10},{10,1... | collective-permute-start | bytes 663560 | tf_op jit(solution)/shard_map/ppermute | solution.py:46
  239.9 12.9 %collective-permute-start.62 = (bf16[144,1024]{1,0:T(8,128)(2,1)S(1)}, bf16[144,1024]{1,0:T(8,128)(2,1)S(1)}, u32[]{:S(2)}, u32[]{:S(2)}) collective-permute-start(bf16[144,1024]{1,0:T(8,128)(2,1)S(1)} %get-tuple-element.197), channel_id=1, source_target_pairs={{0,224},{32,0},{64,32},{96,64},{128,96},{160,128},{192,160},{224,1... | collective-permute-start | bytes 884744 | tf_op jit(solution)/shard_map/ppermute | solution.py:46
  240.0 15.4 %collective-permute-start.63 = (bf16[144,1024]{1,0:T(8,128)(2,1)S(1)}, bf16[144,1024]{1,0:T(8,128)(2,1)S(1)}, u32[]{:S(2)}, u32[]{:S(2)}) collective-permute-start(bf16[144,1024]{1,0:T(8,128)(2,1)S(1)} %get-tuple-element.198), channel_id=1, source_target_pairs={{0,32},{32,64},{64,96},{96,128},{128,160},{160,192},{192,224},{224... | collective-permute-start | bytes 884744 | tf_op jit(solution)/shard_map/ppermute | solution.py:46
  243.3 14.3 %collective-permute-start.58 = (bf16[144,1024]{1,0:T(8,128)(2,1)S(1)}, bf16[144,1024]{1,0:T(8,128)(2,1)S(1)}, u32[]{:S(2)}, u32[]{:S(2)}) collective-permute-start(bf16[144,1024]{1,0:T(8,128)(2,1)S(1)} %down1.1), channel_id=1, source_target_pairs={{0,128},{32,160},{64,192},{96,224},{128,0},{160,32},{192,64},{224,... | collective-permute-start | bytes 884744 | tf_op jit(solution)/shard_map/ppermute | solution.py:46
  246.5 20.6 %collective-permute-start.53 = (bf16[144,1024]{1,0:T(8,128)(2,1)S(1)}, bf16[144,1024]{1,0:T(8,128)(2,1)S(1)}, u32[]{:S(2)}, u32[]{:S(2)}) collective-permute-start(bf16[144,1024]{1,0:T(8,128)(2,1)S(1)} %get-tuple-element.184), channel_id=1, source_target_pairs={{0,160},{32,192},{64,224},{96,0},{128,32},{160,64},{192,96},{224,1... | collective-permute-start | bytes 884744 | tf_op jit(solution)/shard_map/ppermute | solution.py:46
  250.1 20.3 %collective-permute-start.54 = (bf16[144,1024]{1,0:T(8,128)(2,1)S(1)}, bf16[144,1024]{1,0:T(8,128)(2,1)S(1)}, u32[]{:S(2)}, u32[]{:S(2)}) collective-permute-start(bf16[144,1024]{1,0:T(8,128)(2,1)S(1)} %get-tuple-element.185), channel_id=1, source_target_pairs={{0,96},{32,128},{64,160},{96,192},{128,224},{160,0},{192,32},{224,... | collective-permute-start | bytes 884744 | tf_op jit(solution)/shard_map/ppermute | solution.py:46
  252.7 37.6 %collective-permute-start.40 = (bf16[144,1024]{1,0:T(8,128)(2,1)S(1)}, bf16[144,1024]{1,0:T(8,128)(2,1)S(1)}, u32[]{:S(2)}, u32[]{:S(2)}) collective-permute-start(bf16[144,1024]{1,0:T(8,128)(2,1)S(1)} %get-tuple-element.169), channel_id=1, source_target_pairs={{0,192},{32,224},{64,0},{96,32},{128,64},{160,96},{192,128},{224,1... | collective-permute-start | bytes 884744 | tf_op jit(solution)/shard_map/ppermute | solution.py:46
  255.3 35.0 %collective-permute-start.41 = (bf16[144,1024]{1,0:T(8,128)(2,1)S(1)}, bf16[144,1024]{1,0:T(8,128)(2,1)S(1)}, u32[]{:S(2)}, u32[]{:S(2)}) collective-permute-start(bf16[144,1024]{1,0:T(8,128)(2,1)S(1)} %get-tuple-element.170), channel_id=1, source_target_pairs={{0,64},{32,96},{64,128},{96,160},{128,192},{160,224},{192,0},{224,... | collective-permute-start | bytes 884744 | tf_op jit(solution)/shard_map/ppermute | solution.py:46
  300.4 14.4 %collective-permute-start.65 = (bf16[128,1024]{1,0:T(8,128)(2,1)S(1)}, bf16[128,1024]{1,0:T(8,128)(2,1)S(1)}, u32[]{:S(2)}, u32[]{:S(2)}) collective-permute-start(bf16[128,1024]{1,0:T(8,128)(2,1)S(1)} %get-tuple-element.200), channel_id=1, source_target_pairs={{0,8},{8,16},{16,24},{24,0},{1,9},{9,17},{17,25},{25,1},{2,10},{10... | collective-permute-start | bytes 786440 | tf_op jit(solution)/shard_map/ppermute | solution.py:46
  300.5 14.3 %collective-permute-start.66 = (bf16[128,1024]{1,0:T(8,128)(2,1)S(1)}, bf16[128,1024]{1,0:T(8,128)(2,1)S(1)}, u32[]{:S(2)}, u32[]{:S(2)}) collective-permute-start(bf16[128,1024]{1,0:T(8,128)(2,1)S(1)} %get-tuple-element.201), channel_id=1, source_target_pairs={{0,24},{8,0},{16,8},{24,16},{1,25},{9,1},{17,9},{25,17},{2,26},{10... | collective-permute-start | bytes 786440 | tf_op jit(solution)/shard_map/ppermute | solution.py:46
  303.1 11.7 %collective-permute-start.67 = (bf16[128,1024]{1,0:T(8,128)(2,1)S(1)}, bf16[128,1024]{1,0:T(8,128)(2,1)S(1)}, u32[]{:S(2)}, u32[]{:S(2)}) collective-permute-start(bf16[128,1024]{1,0:T(8,128)(2,1)S(1)} %get-tuple-element.202), channel_id=1, source_target_pairs={{0,16},{8,24},{16,0},{24,8},{1,17},{9,25},{17,1},{25,9},{2,18},{10... | collective-permute-start | bytes 786440 | tf_op jit(solution)/shard_map/ppermute | solution.py:46
  (27 other events, 437.2 us)
